TPU v7x, 128 devices: a whole 4x4x4 slice. The times are simulated.
128 devices in a mesh: tm: 16 (over z, x_hi, core), space: 8 (over x_lo, y).
Axes of the slice: x: 4 (x_hi: 2, x_lo: 2; x = x_hi * 2 + x_lo), y: 4, z: 4, core: 2. Of those that a mesh axis runs over, the one named last changes fastest.
Arguments:
- initial: float32 [128, 128, 2048], P('tm', 'space'), may hold values from -6 to 6
- source: float32 [128, 128, 2048], P('tm', 'space'), may hold values from -3 to 3.3
- diffusivity: float32 [128, 2048], P('space'), may hold values from 0.3 to 1
- growth: float32 [128, 2048], P('space'), may hold values from 0.5 to 4
Outputs:
- solution: float32 [128, 128, 2048], P('tm', 'space')
All inputs are finite; a program needn't handle non-finite values.
Results may differ from a plain program's by a relative error of at most 0.00002.
Values sent between devices are 32-bit elements; how exact they have to be, the bound alone decides.
A program may use at most 64 MiB of HBM per device.

v0:
```python
import jax
import jax.numpy as jnp
from jax import lax
from jax.sharding import PartitionSpec as P

LEVELS = 4


diffusion_number = 0.03
time_step = 0.02


def padded_2(block, sides, width):
    for axis, dim in sides:
        count = lax.axis_size(axis)
        forward = [(i, i + 1) for i in range(count - 1)]
        backward = [(target, source) for source, target in forward]
        low = lax.ppermute(
            lax.slice_in_dim(block, block.shape[dim] - width, None, axis=dim), axis, forward
        )
        high = lax.ppermute(lax.slice_in_dim(block, 0, width, axis=dim), axis, backward)
        block = jnp.concatenate([low, block, high], axis=dim)
    return block


def from_behind(array, axis, by):
    peers = lax.axis_size(axis)
    return lax.ppermute(array, axis, [(i, (i + by) % peers) for i in range(peers)])


def propagate(fields, scales, diffusivity, growth):
    padded = padded_2(fields, (("space", 1),), 1)
    padded = jnp.pad(padded, ((0, 0), (0, 0), (1, 1)))
    beside_all = (
        padded[:, :-2, 1:-1] + padded[:, 2:, 1:-1] + padded[:, 1:-1, :-2] + padded[:, 1:-1, 2:]
    )
    laplace = beside_all - 4.0 * fields
    factor = scales[:, None, None]
    return (
        fields
        + diffusion_number * factor * diffusivity * laplace
        + time_step * factor * growth * fields / (1.0 + fields * fields)
    )


def uniform_scales(count, level_index):
    return jnp.full((count,), 2.0**level_index, jnp.float32)


def previous(points):
    return from_behind(points[-1:], "tm", 1)


def coarsest(states, forcing, diffusivity, growth):
    unit = uniform_scales(1, LEVELS - 1)
    position = lax.axis_index("tm")
    arriving = previous(states)

    def section(index, carry):
        waiting, result = carry
        prior = waiting
        prior = propagate(prior, unit, diffusivity, growth) + forcing
        outputs = [prior]
        fresh = jnp.concatenate(outputs, axis=0)
        result = jnp.where(position == index, fresh, result)
        passed = previous(result)
        waiting = jnp.where(position == index + 1, passed, waiting)
        return (waiting, result)

    arriving, result = lax.fori_loop(0, lax.axis_size("tm"), section, (arriving, states))
    return result


def cycle(level_index, states, forcing, diffusivity, growth):
    if level_index == LEVELS - 1:
        return coarsest(states, forcing, diffusivity, growth)
    half = states.shape[0] // 2
    scales = uniform_scales(half, level_index)
    even_forcing = forcing[0::2]
    odd_forcing = forcing[1::2]
    even_points = states[0::2]
    odd_points = propagate(even_points, scales, diffusivity, growth) + odd_forcing
    shifted = jnp.concatenate([previous(odd_points), odd_points[:-1]], axis=0)
    even_points = propagate(shifted, scales, diffusivity, growth) + even_forcing
    odd_points = propagate(even_points, scales, diffusivity, growth) + odd_forcing
    both_scales = jnp.concatenate([scales, uniform_scales(half, level_index + 1)])
    images = propagate(
        jnp.concatenate([odd_points, even_points], axis=0), both_scales, diffusivity, growth
    )
    pair_terms = images[:half] - images[half:]
    reduced_forcing = even_forcing + jnp.concatenate(
        [previous(pair_terms), pair_terms[:-1]], axis=0
    )
    coarse_points = cycle(level_index + 1, even_points, reduced_forcing, diffusivity, growth)
    odd_points = propagate(coarse_points, scales, diffusivity, growth) + odd_forcing
    return jnp.stack([coarse_points, odd_points], axis=1).reshape(states.shape)


def body(initial, source, diffusivity, growth):
    return cycle(0, initial, source, diffusivity, growth)


def solution(mesh):
    placed = (P("tm", "space", None), P("tm", "space", None), P("space", None), P("space", None))
    return jax.shard_map(
        body, mesh=mesh, in_specs=placed, out_specs=P("tm", "space", None), check_vma=False
    )
```

profile of v0, /device:TPU:24, one launch (start us, length us, event | category | flops | bytes accessed | tf_op | source)
XLA Modules:
  0.0 496.4 jit_solution(10565957976021507318)
XLA Ops:
  13.3 8.0 %collective-permute-done.5 = f32[1,16,2048]{2,1,0:T(8,128)S(1)} collective-permute-done((f32[1,16,2048]{2,1,0:T(8,128)S(1)}, f32[1,16,2048]{2,1,0:T(8,128)S(1)}, u32[]{:S(2)}, u32[]{:S(2)}) %collective-permute-start.5) | collective-permute-done | bytes 131104 | tf_op jit(solution)/shard_map/ppermute | solution.py:28
  65.5 8.0 %collective-permute-done.15 = f32[1,16,2048]{2,1,0:T(8,128)S(1)} collective-permute-done((f32[1,16,2048]{2,1,0:T(8,128)S(1)}, f32[1,16,2048]{2,1,0:T(8,128)S(1)}, u32[]{:S(2)}, u32[]{:S(2)}) %collective-permute-start.15) | collective-permute-done | bytes 131104 | tf_op jit(solution)/shard_map/ppermute | solution.py:28
  119.5 8.0 %collective-permute-done.25 = f32[1,16,2048]{2,1,0:T(8,128)S(1)} collective-permute-done((f32[1,16,2048]{2,1,0:T(8,128)S(1)}, f32[1,16,2048]{2,1,0:T(8,128)S(1)}, u32[]{:S(2)}, u32[]{:S(2)}) %collective-permute-start.25) | collective-permute-done | bytes 131104 | tf_op jit(solution)/shard_map/ppermute | solution.py:28
  161.8 7.9 %collective-permute-done.33 = f32[1,16,2048]{2,1,0:T(8,128)S(1)} collective-permute-done((f32[1,16,2048]{2,1,0:T(8,128)S(1)}, f32[1,16,2048]{2,1,0:T(8,128)S(1)}, u32[]{:S(2)}, u32[]{:S(2)}) %collective-permute-start.33) | collective-permute-done | bytes 131104 | tf_op jit(solution)/shard_map/ppermute | solution.py:28
  171.1 288.6 %while.17 = (s32[]{:T(128)}, f32[1,16,2048]{2,1,0:T(8,128)S(1)}, f32[1,16,2048]{2,1,0:T(8,128)S(1)}, s32[]{:T(128)}, f32[16,2048]{1,0:T(8,128)S(1)}, /*index=5*/...) while((s32[]{:T(128)}, f32[1,16,2048]{2,1,0:T(8,128)S(1)}, f32[1,16,2048]{2,1,0:T(8,128)S(1)}, ...), condition=%wide.region_1.2_spmd, body=%wide.region_0.1_spmd.sunk | while | flops 917796 | bytes 2376049 | solution.py:70
  180.9 8.0 %collective-permute-done.2 = f32[1,16,2048]{2,1,0:T(8,128)S(1)} collective-permute-done((f32[1,16,2048]{2,1,0:T(8,128)S(1)}, f32[1,16,2048]{2,1,0:T(8,128)S(1)}, u32[]{:S(2)}, u32[]{:S(2)}) %collective-permute-start.2) | collective-permute-done | bytes 131104 | tf_op jit(solution)/shard_map/while/body/eval_jaxpr/ppermute | solution.py:28
  190.9 6.3 %collective-permute-start.1 = (f32[1,1,2048]{2,1,0:T(1,128)S(1)}, f32[1,1,2048]{2,1,0:T(1,128)S(1)}, u32[]{:S(2)}, u32[]{:S(2)}) collective-permute-start(f32[1,1,2048]{2,1,0:T(1,128)S(1)} %get-tuple-element.286), channel_id=1, source_target_pairs={{0,1},{1,2},{2,3},{3,4},{4,5},{5,6},{6,7},{8,9},{9,10},{10,11},{11... | collective-permute-start | bytes 24584 | tf_op jit(solution)/shard_map/while/body/eval_jaxpr/ppermute | solution.py:18
  198.9 8.0 %collective-permute-done.2 = f32[1,16,2048]{2,1,0:T(8,128)S(1)} collective-permute-done((f32[1,16,2048]{2,1,0:T(8,128)S(1)}, f32[1,16,2048]{2,1,0:T(8,128)S(1)}, u32[]{:S(2)}, u32[]{:S(2)}) %collective-permute-start.2) | collective-permute-done | bytes 131104 | tf_op jit(solution)/shard_map/while/body/eval_jaxpr/ppermute | solution.py:28
  208.9 6.3 %collective-permute-start.1 = (f32[1,1,2048]{2,1,0:T(1,128)S(1)}, f32[1,1,2048]{2,1,0:T(1,128)S(1)}, u32[]{:S(2)}, u32[]{:S(2)}) collective-permute-start(f32[1,1,2048]{2,1,0:T(1,128)S(1)} %get-tuple-element.286), channel_id=1, source_target_pairs={{0,1},{1,2},{2,3},{3,4},{4,5},{5,6},{6,7},{8,9},{9,10},{10,11},{11... | collective-permute-start | bytes 24584 | tf_op jit(solution)/shard_map/while/body/eval_jaxpr/ppermute | solution.py:18
  217.0 8.0 %collective-permute-done.2 = f32[1,16,2048]{2,1,0:T(8,128)S(1)} collective-permute-done((f32[1,16,2048]{2,1,0:T(8,128)S(1)}, f32[1,16,2048]{2,1,0:T(8,128)S(1)}, u32[]{:S(2)}, u32[]{:S(2)}) %collective-permute-start.2) | collective-permute-done | bytes 131104 | tf_op jit(solution)/shard_map/while/body/eval_jaxpr/ppermute | solution.py:28
  227.0 6.3 %collective-permute-start.1 = (f32[1,1,2048]{2,1,0:T(1,128)S(1)}, f32[1,1,2048]{2,1,0:T(1,128)S(1)}, u32[]{:S(2)}, u32[]{:S(2)}) collective-permute-start(f32[1,1,2048]{2,1,0:T(1,128)S(1)} %get-tuple-element.286), channel_id=1, source_target_pairs={{0,1},{1,2},{2,3},{3,4},{4,5},{5,6},{6,7},{8,9},{9,10},{10,11},{11... | collective-permute-start | bytes 24584 | tf_op jit(solution)/shard_map/while/body/eval_jaxpr/ppermute | solution.py:18
  235.1 8.0 %collective-permute-done.2 = f32[1,16,2048]{2,1,0:T(8,128)S(1)} collective-permute-done((f32[1,16,2048]{2,1,0:T(8,128)S(1)}, f32[1,16,2048]{2,1,0:T(8,128)S(1)}, u32[]{:S(2)}, u32[]{:S(2)}) %collective-permute-start.2) | collective-permute-done | bytes 131104 | tf_op jit(solution)/shard_map/while/body/eval_jaxpr/ppermute | solution.py:28
  245.0 6.3 %collective-permute-start.1 = (f32[1,1,2048]{2,1,0:T(1,128)S(1)}, f32[1,1,2048]{2,1,0:T(1,128)S(1)}, u32[]{:S(2)}, u32[]{:S(2)}) collective-permute-start(f32[1,1,2048]{2,1,0:T(1,128)S(1)} %get-tuple-element.286), channel_id=1, source_target_pairs={{0,1},{1,2},{2,3},{3,4},{4,5},{5,6},{6,7},{8,9},{9,10},{10,11},{11... | collective-permute-start | bytes 24584 | tf_op jit(solution)/shard_map/while/body/eval_jaxpr/ppermute | solution.py:18
  253.1 8.0 %collective-permute-done.2 = f32[1,16,2048]{2,1,0:T(8,128)S(1)} collective-permute-done((f32[1,16,2048]{2,1,0:T(8,128)S(1)}, f32[1,16,2048]{2,1,0:T(8,128)S(1)}, u32[]{:S(2)}, u32[]{:S(2)}) %collective-permute-start.2) | collective-permute-done | bytes 131104 | tf_op jit(solution)/shard_map/while/body/eval_jaxpr/ppermute | solution.py:28
  263.1 6.3 %collective-permute-start.1 = (f32[1,1,2048]{2,1,0:T(1,128)S(1)}, f32[1,1,2048]{2,1,0:T(1,128)S(1)}, u32[]{:S(2)}, u32[]{:S(2)}) collective-permute-start(f32[1,1,2048]{2,1,0:T(1,128)S(1)} %get-tuple-element.286), channel_id=1, source_target_pairs={{0,1},{1,2},{2,3},{3,4},{4,5},{5,6},{6,7},{8,9},{9,10},{10,11},{11... | collective-permute-start | bytes 24584 | tf_op jit(solution)/shard_map/while/body/eval_jaxpr/ppermute | solution.py:18
  271.2 8.0 %collective-permute-done.2 = f32[1,16,2048]{2,1,0:T(8,128)S(1)} collective-permute-done((f32[1,16,2048]{2,1,0:T(8,128)S(1)}, f32[1,16,2048]{2,1,0:T(8,128)S(1)}, u32[]{:S(2)}, u32[]{:S(2)}) %collective-permute-start.2) | collective-permute-done | bytes 131104 | tf_op jit(solution)/shard_map/while/body/eval_jaxpr/ppermute | solution.py:28
  281.1 6.3 %collective-permute-start.1 = (f32[1,1,2048]{2,1,0:T(1,128)S(1)}, f32[1,1,2048]{2,1,0:T(1,128)S(1)}, u32[]{:S(2)}, u32[]{:S(2)}) collective-permute-start(f32[1,1,2048]{2,1,0:T(1,128)S(1)} %get-tuple-element.286), channel_id=1, source_target_pairs={{0,1},{1,2},{2,3},{3,4},{4,5},{5,6},{6,7},{8,9},{9,10},{10,11},{11... | collective-permute-start | bytes 24584 | tf_op jit(solution)/shard_map/while/body/eval_jaxpr/ppermute | solution.py:18
  289.2 8.0 %collective-permute-done.2 = f32[1,16,2048]{2,1,0:T(8,128)S(1)} collective-permute-done((f32[1,16,2048]{2,1,0:T(8,128)S(1)}, f32[1,16,2048]{2,1,0:T(8,128)S(1)}, u32[]{:S(2)}, u32[]{:S(2)}) %collective-permute-start.2) | collective-permute-done | bytes 131104 | tf_op jit(solution)/shard_map/while/body/eval_jaxpr/ppermute | solution.py:28
  299.2 6.3 %collective-permute-start.1 = (f32[1,1,2048]{2,1,0:T(1,128)S(1)}, f32[1,1,2048]{2,1,0:T(1,128)S(1)}, u32[]{:S(2)}, u32[]{:S(2)}) collective-permute-start(f32[1,1,2048]{2,1,0:T(1,128)S(1)} %get-tuple-element.286), channel_id=1, source_target_pairs={{0,1},{1,2},{2,3},{3,4},{4,5},{5,6},{6,7},{8,9},{9,10},{10,11},{11... | collective-permute-start | bytes 24584 | tf_op jit(solution)/shard_map/while/body/eval_jaxpr/ppermute | solution.py:18
  307.3 8.0 %collective-permute-done.2 = f32[1,16,2048]{2,1,0:T(8,128)S(1)} collective-permute-done((f32[1,16,2048]{2,1,0:T(8,128)S(1)}, f32[1,16,2048]{2,1,0:T(8,128)S(1)}, u32[]{:S(2)}, u32[]{:S(2)}) %collective-permute-start.2) | collective-permute-done | bytes 131104 | tf_op jit(solution)/shard_map/while/body/eval_jaxpr/ppermute | solution.py:28
  317.3 6.3 %collective-permute-start.1 = (f32[1,1,2048]{2,1,0:T(1,128)S(1)}, f32[1,1,2048]{2,1,0:T(1,128)S(1)}, u32[]{:S(2)}, u32[]{:S(2)}) collective-permute-start(f32[1,1,2048]{2,1,0:T(1,128)S(1)} %get-tuple-element.286), channel_id=1, source_target_pairs={{0,1},{1,2},{2,3},{3,4},{4,5},{5,6},{6,7},{8,9},{9,10},{10,11},{11... | collective-permute-start | bytes 24584 | tf_op jit(solution)/shard_map/while/body/eval_jaxpr/ppermute | solution.py:18
  325.3 8.0 %collective-permute-done.2 = f32[1,16,2048]{2,1,0:T(8,128)S(1)} collective-permute-done((f32[1,16,2048]{2,1,0:T(8,128)S(1)}, f32[1,16,2048]{2,1,0:T(8,128)S(1)}, u32[]{:S(2)}, u32[]{:S(2)}) %collective-permute-start.2) | collective-permute-done | bytes 131104 | tf_op jit(solution)/shard_map/while/body/eval_jaxpr/ppermute | solution.py:28
  343.4 8.0 %collective-permute-done.2 = f32[1,16,2048]{2,1,0:T(8,128)S(1)} collective-permute-done((f32[1,16,2048]{2,1,0:T(8,128)S(1)}, f32[1,16,2048]{2,1,0:T(8,128)S(1)}, u32[]{:S(2)}, u32[]{:S(2)}) %collective-permute-start.2) | collective-permute-done | bytes 131104 | tf_op jit(solution)/shard_map/while/body/eval_jaxpr/ppermute | solution.py:28
  353.4 6.3 %collective-permute-start.1 = (f32[1,1,2048]{2,1,0:T(1,128)S(1)}, f32[1,1,2048]{2,1,0:T(1,128)S(1)}, u32[]{:S(2)}, u32[]{:S(2)}) collective-permute-start(f32[1,1,2048]{2,1,0:T(1,128)S(1)} %get-tuple-element.286), channel_id=1, source_target_pairs={{0,1},{1,2},{2,3},{3,4},{4,5},{5,6},{6,7},{8,9},{9,10},{10,11},{11... | collective-permute-start | bytes 24584 | tf_op jit(solution)/shard_map/while/body/eval_jaxpr/ppermute | solution.py:18
  361.4 8.0 %collective-permute-done.2 = f32[1,16,2048]{2,1,0:T(8,128)S(1)} collective-permute-done((f32[1,16,2048]{2,1,0:T(8,128)S(1)}, f32[1,16,2048]{2,1,0:T(8,128)S(1)}, u32[]{:S(2)}, u32[]{:S(2)}) %collective-permute-start.2) | collective-permute-done | bytes 131104 | tf_op jit(solution)/shard_map/while/body/eval_jaxpr/ppermute | solution.py:28
  379.5 8.0 %collective-permute-done.2 = f32[1,16,2048]{2,1,0:T(8,128)S(1)} collective-permute-done((f32[1,16,2048]{2,1,0:T(8,128)S(1)}, f32[1,16,2048]{2,1,0:T(8,128)S(1)}, u32[]{:S(2)}, u32[]{:S(2)}) %collective-permute-start.2) | collective-permute-done | bytes 131104 | tf_op jit(solution)/shard_map/while/body/eval_jaxpr/ppermute | solution.py:28
  397.6 8.0 %collective-permute-done.2 = f32[1,16,2048]{2,1,0:T(8,128)S(1)} collective-permute-done((f32[1,16,2048]{2,1,0:T(8,128)S(1)}, f32[1,16,2048]{2,1,0:T(8,128)S(1)}, u32[]{:S(2)}, u32[]{:S(2)}) %collective-permute-start.2) | collective-permute-done | bytes 131104 | tf_op jit(solution)/shard_map/while/body/eval_jaxpr/ppermute | solution.py:28
  415.6 8.0 %collective-permute-done.2 = f32[1,16,2048]{2,1,0:T(8,128)S(1)} collective-permute-done((f32[1,16,2048]{2,1,0:T(8,128)S(1)}, f32[1,16,2048]{2,1,0:T(8,128)S(1)}, u32[]{:S(2)}, u32[]{:S(2)}) %collective-permute-start.2) | collective-permute-done | bytes 131104 | tf_op jit(solution)/shard_map/while/body/eval_jaxpr/ppermute | solution.py:28
  425.6 6.3 %collective-permute-start.1 = (f32[1,1,2048]{2,1,0:T(1,128)S(1)}, f32[1,1,2048]{2,1,0:T(1,128)S(1)}, u32[]{:S(2)}, u32[]{:S(2)}) collective-permute-start(f32[1,1,2048]{2,1,0:T(1,128)S(1)} %get-tuple-element.286), channel_id=1, source_target_pairs={{0,1},{1,2},{2,3},{3,4},{4,5},{5,6},{6,7},{8,9},{9,10},{10,11},{11... | collective-permute-start | bytes 24584 | tf_op jit(solution)/shard_map/while/body/eval_jaxpr/ppermute | solution.py:18
  433.7 8.0 %collective-permute-done.2 = f32[1,16,2048]{2,1,0:T(8,128)S(1)} collective-permute-done((f32[1,16,2048]{2,1,0:T(8,128)S(1)}, f32[1,16,2048]{2,1,0:T(8,128)S(1)}, u32[]{:S(2)}, u32[]{:S(2)}) %collective-permute-start.2) | collective-permute-done | bytes 131104 | tf_op jit(solution)/shard_map/while/body/eval_jaxpr/ppermute | solution.py:28
  443.7 6.3 %collective-permute-start.1 = (f32[1,1,2048]{2,1,0:T(1,128)S(1)}, f32[1,1,2048]{2,1,0:T(1,128)S(1)}, u32[]{:S(2)}, u32[]{:S(2)}) collective-permute-start(f32[1,1,2048]{2,1,0:T(1,128)S(1)} %get-tuple-element.286), channel_id=1, source_target_pairs={{0,1},{1,2},{2,3},{3,4},{4,5},{5,6},{6,7},{8,9},{9,10},{10,11},{11... | collective-permute-start | bytes 24584 | tf_op jit(solution)/shard_map/while/body/eval_jaxpr/ppermute | solution.py:18
  451.7 8.0 %collective-permute-done.2 = f32[1,16,2048]{2,1,0:T(8,128)S(1)} collective-permute-done((f32[1,16,2048]{2,1,0:T(8,128)S(1)}, f32[1,16,2048]{2,1,0:T(8,128)S(1)}, u32[]{:S(2)}, u32[]{:S(2)}) %collective-permute-start.2) | collective-permute-done | bytes 131104 | tf_op jit(solution)/shard_map/while/body/eval_jaxpr/ppermute | solution.py:28
  (287 shorter events, 265.2 us)
Async XLA Ops:
  13.2 8.1 %collective-permute-start.5 = (f32[1,16,2048]{2,1,0:T(8,128)S(1)}, f32[1,16,2048]{2,1,0:T(8,128)S(1)}, u32[]{:S(2)}, u32[]{:S(2)}) collective-permute-start(f32[1,16,2048]{2,1,0:T(8,128)S(1)} %slice.587), channel_id=1, source_target_pairs={{0,8},{8,16},{16,24},{24,32},{32,40},{40,48},{48,56},{56,64},{64,7... | collective-permute-start | bytes 393224 | tf_op jit(solution)/shard_map/ppermute | solution.py:28
  43.0 12.0 %collective-permute-start.12 = (f32[8,1,2048]{2,1,0:T(1,128)S(1)}, f32[8,1,2048]{2,1,0:T(1,128)S(1)}, u32[]{:S(2)}, u32[]{:S(2)}) collective-permute-start(f32[8,1,2048]{2,1,0:T(1,128)S(1)} %get-tuple-element.198), channel_id=1, source_target_pairs={{0,1},{1,2},{2,3},{3,4},{4,5},{5,6},{6,7},{8,9},{9,10},{10,11},{11... | collective-permute-start | bytes 196616 | tf_op jit(solution)/shard_map/ppermute | solution.py:18
  45.1 9.9 %collective-permute-start.13 = (f32[8,1,2048]{2,1,0:T(1,128)S(1)}, f32[8,1,2048]{2,1,0:T(1,128)S(1)}, u32[]{:S(2)}, u32[]{:S(2)}) collective-permute-start(f32[8,1,2048]{2,1,0:T(1,128)S(1)} %get-tuple-element.199), channel_id=1, source_target_pairs={{1,0},{2,1},{3,2},{4,3},{5,4},{6,5},{7,6},{9,8},{10,9},{11,10},{12... | collective-permute-start | bytes 196616 | tf_op jit(solution)/shard_map/ppermute | solution.py:21
  57.0 8.1 %collective-permute-start.14 = (f32[1,16,2048]{2,1,0:T(8,128)S(1)}, f32[1,16,2048]{2,1,0:T(8,128)S(1)}, u32[]{:S(2)}, u32[]{:S(2)}) collective-permute-start(f32[1,16,2048]{2,1,0:T(8,128)S(1)} %slice.611), channel_id=1, source_target_pairs={{0,8},{8,16},{16,24},{24,32},{32,40},{40,48},{48,56},{56,64},{64,7... | collective-permute-start | bytes 393224 | tf_op jit(solution)/shard_map/ppermute | solution.py:28
  98.2 11.9 %collective-permute-start.22 = (f32[4,1,2048]{2,1,0:T(1,128)S(1)}, f32[4,1,2048]{2,1,0:T(1,128)S(1)}, u32[]{:S(2)}, u32[]{:S(2)}) collective-permute-start(f32[4,1,2048]{2,1,0:T(1,128)S(1)} %get-tuple-element.202), channel_id=1, source_target_pairs={{0,1},{1,2},{2,3},{3,4},{4,5},{5,6},{6,7},{8,9},{9,10},{10,11},{11... | collective-permute-start | bytes 98312 | tf_op jit(solution)/shard_map/ppermute | solution.py:18
  100.2 9.9 %collective-permute-start.23 = (f32[4,1,2048]{2,1,0:T(1,128)S(1)}, f32[4,1,2048]{2,1,0:T(1,128)S(1)}, u32[]{:S(2)}, u32[]{:S(2)}) collective-permute-start(f32[4,1,2048]{2,1,0:T(1,128)S(1)} %get-tuple-element.203), channel_id=1, source_target_pairs={{1,0},{2,1},{3,2},{4,3},{5,4},{6,5},{7,6},{9,8},{10,9},{11,10},{12... | collective-permute-start | bytes 98312 | tf_op jit(solution)/shard_map/ppermute | solution.py:21
  111.1 8.1 %collective-permute-start.24 = (f32[1,16,2048]{2,1,0:T(8,128)S(1)}, f32[1,16,2048]{2,1,0:T(8,128)S(1)}, u32[]{:S(2)}, u32[]{:S(2)}) collective-permute-start(f32[1,16,2048]{2,1,0:T(8,128)S(1)} %get-tuple-element.216), channel_id=1, source_target_pairs={{0,8},{8,16},{16,24},{24,32},{32,40},{40,48},{48,56},{56,64},{64,7... | collective-permute-start | bytes 393224 | tf_op jit(solution)/shard_map/ppermute | solution.py:28
  119.4 8.1 %collective-permute-start.25 = (f32[1,16,2048]{2,1,0:T(8,128)S(1)}, f32[1,16,2048]{2,1,0:T(8,128)S(1)}, u32[]{:S(2)}, u32[]{:S(2)}) collective-permute-start(f32[1,16,2048]{2,1,0:T(8,128)S(1)} %fusion.113), channel_id=1, source_target_pairs={{0,8},{8,16},{16,24},{24,32},{32,40},{40,48},{48,56},{56,64},{64,7... | collective-permute-start | bytes 393224 | tf_op jit(solution)/shard_map/ppermute | solution.py:28
  161.7 9.4 %collective-permute-start.28 = (f32[1,16,2048]{2,1,0:T(8,128)S(1)}, f32[1,16,2048]{2,1,0:T(8,128)S(1)}, u32[]{:S(2)}, u32[]{:S(2)}) collective-permute-start(f32[1,16,2048]{2,1,0:T(8,128)S(1)} %fusion.107), channel_id=1, source_target_pairs={{0,8},{8,16},{16,24},{24,32},{32,40},{40,48},{48,56},{56,64},{64,7... | collective-permute-start | bytes 393224 | tf_op jit(solution)/shard_map/ppermute | solution.py:28
  188.9 8.2 %collective-permute-start = (f32[1,1,2048]{2,1,0:T(1,128)S(1)}, f32[1,1,2048]{2,1,0:T(1,128)S(1)}, u32[]{:S(2)}, u32[]{:S(2)}) collective-permute-start(f32[1,1,2048]{2,1,0:T(1,128)S(1)} %get-tuple-element.285), channel_id=1, source_target_pairs={{1,0},{2,1},{3,2},{4,3},{5,4},{6,5},{7,6},{9,8},{10,9},{11,10},{12... | collective-permute-start | bytes 24584 | tf_op jit(solution)/shard_map/while/body/eval_jaxpr/ppermute | solution.py:21
  198.9 8.1 %collective-permute-start.2 = (f32[1,16,2048]{2,1,0:T(8,128)S(1)}, f32[1,16,2048]{2,1,0:T(8,128)S(1)}, u32[]{:S(2)}, u32[]{:S(2)}) collective-permute-start(f32[1,16,2048]{2,1,0:T(8,128)S(1)} %fusion.145), channel_id=1, source_target_pairs={{0,8},{8,16},{16,24},{24,32},{32,40},{40,48},{48,56},{56,64},{64,7... | collective-permute-start | bytes 393224 | tf_op jit(solution)/shard_map/while/body/eval_jaxpr/ppermute | solution.py:28
  207.0 8.2 %collective-permute-start = (f32[1,1,2048]{2,1,0:T(1,128)S(1)}, f32[1,1,2048]{2,1,0:T(1,128)S(1)}, u32[]{:S(2)}, u32[]{:S(2)}) collective-permute-start(f32[1,1,2048]{2,1,0:T(1,128)S(1)} %get-tuple-element.285), channel_id=1, source_target_pairs={{1,0},{2,1},{3,2},{4,3},{5,4},{6,5},{7,6},{9,8},{10,9},{11,10},{12... | collective-permute-start | bytes 24584 | tf_op jit(solution)/shard_map/while/body/eval_jaxpr/ppermute | solution.py:21
  216.9 8.1 %collective-permute-start.2 = (f32[1,16,2048]{2,1,0:T(8,128)S(1)}, f32[1,16,2048]{2,1,0:T(8,128)S(1)}, u32[]{:S(2)}, u32[]{:S(2)}) collective-permute-start(f32[1,16,2048]{2,1,0:T(8,128)S(1)} %fusion.145), channel_id=1, source_target_pairs={{0,8},{8,16},{16,24},{24,32},{32,40},{40,48},{48,56},{56,64},{64,7... | collective-permute-start | bytes 393224 | tf_op jit(solution)/shard_map/while/body/eval_jaxpr/ppermute | solution.py:28
  225.1 8.2 %collective-permute-start = (f32[1,1,2048]{2,1,0:T(1,128)S(1)}, f32[1,1,2048]{2,1,0:T(1,128)S(1)}, u32[]{:S(2)}, u32[]{:S(2)}) collective-permute-start(f32[1,1,2048]{2,1,0:T(1,128)S(1)} %get-tuple-element.285), channel_id=1, source_target_pairs={{1,0},{2,1},{3,2},{4,3},{5,4},{6,5},{7,6},{9,8},{10,9},{11,10},{12... | collective-permute-start | bytes 24584 | tf_op jit(solution)/shard_map/while/body/eval_jaxpr/ppermute | solution.py:21
  235.0 8.1 %collective-permute-start.2 = (f32[1,16,2048]{2,1,0:T(8,128)S(1)}, f32[1,16,2048]{2,1,0:T(8,128)S(1)}, u32[]{:S(2)}, u32[]{:S(2)}) collective-permute-start(f32[1,16,2048]{2,1,0:T(8,128)S(1)} %fusion.145), channel_id=1, source_target_pairs={{0,8},{8,16},{16,24},{24,32},{32,40},{40,48},{48,56},{56,64},{64,7... | collective-permute-start | bytes 393224 | tf_op jit(solution)/shard_map/while/body/eval_jaxpr/ppermute | solution.py:28
  243.1 8.2 %collective-permute-start = (f32[1,1,2048]{2,1,0:T(1,128)S(1)}, f32[1,1,2048]{2,1,0:T(1,128)S(1)}, u32[]{:S(2)}, u32[]{:S(2)}) collective-permute-start(f32[1,1,2048]{2,1,0:T(1,128)S(1)} %get-tuple-element.285), channel_id=1, source_target_pairs={{1,0},{2,1},{3,2},{4,3},{5,4},{6,5},{7,6},{9,8},{10,9},{11,10},{12... | collective-permute-start | bytes 24584 | tf_op jit(solution)/shard_map/while/body/eval_jaxpr/ppermute | solution.py:21
  261.2 8.2 %collective-permute-start = (f32[1,1,2048]{2,1,0:T(1,128)S(1)}, f32[1,1,2048]{2,1,0:T(1,128)S(1)}, u32[]{:S(2)}, u32[]{:S(2)}) collective-permute-start(f32[1,1,2048]{2,1,0:T(1,128)S(1)} %get-tuple-element.285), channel_id=1, source_target_pairs={{1,0},{2,1},{3,2},{4,3},{5,4},{6,5},{7,6},{9,8},{10,9},{11,10},{12... | collective-permute-start | bytes 24584 | tf_op jit(solution)/shard_map/while/body/eval_jaxpr/ppermute | solution.py:21
  279.2 8.2 %collective-permute-start = (f32[1,1,2048]{2,1,0:T(1,128)S(1)}, f32[1,1,2048]{2,1,0:T(1,128)S(1)}, u32[]{:S(2)}, u32[]{:S(2)}) collective-permute-start(f32[1,1,2048]{2,1,0:T(1,128)S(1)} %get-tuple-element.285), channel_id=1, source_target_pairs={{1,0},{2,1},{3,2},{4,3},{5,4},{6,5},{7,6},{9,8},{10,9},{11,10},{12... | collective-permute-start | bytes 24584 | tf_op jit(solution)/shard_map/while/body/eval_jaxpr/ppermute | solution.py:21
  289.1 8.1 %collective-permute-start.2 = (f32[1,16,2048]{2,1,0:T(8,128)S(1)}, f32[1,16,2048]{2,1,0:T(8,128)S(1)}, u32[]{:S(2)}, u32[]{:S(2)}) collective-permute-start(f32[1,16,2048]{2,1,0:T(8,128)S(1)} %fusion.145), channel_id=1, source_target_pairs={{0,8},{8,16},{16,24},{24,32},{32,40},{40,48},{48,56},{56,64},{64,7... | collective-permute-start | bytes 393224 | tf_op jit(solution)/shard_map/while/body/eval_jaxpr/ppermute | solution.py:28
  297.3 8.2 %collective-permute-start = (f32[1,1,2048]{2,1,0:T(1,128)S(1)}, f32[1,1,2048]{2,1,0:T(1,128)S(1)}, u32[]{:S(2)}, u32[]{:S(2)}) collective-permute-start(f32[1,1,2048]{2,1,0:T(1,128)S(1)} %get-tuple-element.285), channel_id=1, source_target_pairs={{1,0},{2,1},{3,2},{4,3},{5,4},{6,5},{7,6},{9,8},{10,9},{11,10},{12... | collective-permute-start | bytes 24584 | tf_op jit(solution)/shard_map/while/body/eval_jaxpr/ppermute | solution.py:21
  307.2 8.1 %collective-permute-start.2 = (f32[1,16,2048]{2,1,0:T(8,128)S(1)}, f32[1,16,2048]{2,1,0:T(8,128)S(1)}, u32[]{:S(2)}, u32[]{:S(2)}) collective-permute-start(f32[1,16,2048]{2,1,0:T(8,128)S(1)} %fusion.145), channel_id=1, source_target_pairs={{0,8},{8,16},{16,24},{24,32},{32,40},{40,48},{48,56},{56,64},{64,7... | collective-permute-start | bytes 393224 | tf_op jit(solution)/shard_map/while/body/eval_jaxpr/ppermute | solution.py:28
  315.3 8.2 %collective-permute-start = (f32[1,1,2048]{2,1,0:T(1,128)S(1)}, f32[1,1,2048]{2,1,0:T(1,128)S(1)}, u32[]{:S(2)}, u32[]{:S(2)}) collective-permute-start(f32[1,1,2048]{2,1,0:T(1,128)S(1)} %get-tuple-element.285), channel_id=1, source_target_pairs={{1,0},{2,1},{3,2},{4,3},{5,4},{6,5},{7,6},{9,8},{10,9},{11,10},{12... | collective-permute-start | bytes 24584 | tf_op jit(solution)/shard_map/while/body/eval_jaxpr/ppermute | solution.py:21
  333.4 8.2 %collective-permute-start = (f32[1,1,2048]{2,1,0:T(1,128)S(1)}, f32[1,1,2048]{2,1,0:T(1,128)S(1)}, u32[]{:S(2)}, u32[]{:S(2)}) collective-permute-start(f32[1,1,2048]{2,1,0:T(1,128)S(1)} %get-tuple-element.285), channel_id=1, source_target_pairs={{1,0},{2,1},{3,2},{4,3},{5,4},{6,5},{7,6},{9,8},{10,9},{11,10},{12... | collective-permute-start | bytes 24584 | tf_op jit(solution)/shard_map/while/body/eval_jaxpr/ppermute | solution.py:21
  351.4 8.2 %collective-permute-start = (f32[1,1,2048]{2,1,0:T(1,128)S(1)}, f32[1,1,2048]{2,1,0:T(1,128)S(1)}, u32[]{:S(2)}, u32[]{:S(2)}) collective-permute-start(f32[1,1,2048]{2,1,0:T(1,128)S(1)} %get-tuple-element.285), channel_id=1, source_target_pairs={{1,0},{2,1},{3,2},{4,3},{5,4},{6,5},{7,6},{9,8},{10,9},{11,10},{12... | collective-permute-start | bytes 24584 | tf_op jit(solution)/shard_map/while/body/eval_jaxpr/ppermute | solution.py:21
  369.5 8.2 %collective-permute-start = (f32[1,1,2048]{2,1,0:T(1,128)S(1)}, f32[1,1,2048]{2,1,0:T(1,128)S(1)}, u32[]{:S(2)}, u32[]{:S(2)}) collective-permute-start(f32[1,1,2048]{2,1,0:T(1,128)S(1)} %get-tuple-element.285), channel_id=1, source_target_pairs={{1,0},{2,1},{3,2},{4,3},{5,4},{6,5},{7,6},{9,8},{10,9},{11,10},{12... | collective-permute-start | bytes 24584 | tf_op jit(solution)/shard_map/while/body/eval_jaxpr/ppermute | solution.py:21
  379.4 8.1 %collective-permute-start.2 = (f32[1,16,2048]{2,1,0:T(8,128)S(1)}, f32[1,16,2048]{2,1,0:T(8,128)S(1)}, u32[]{:S(2)}, u32[]{:S(2)}) collective-permute-start(f32[1,16,2048]{2,1,0:T(8,128)S(1)} %fusion.145), channel_id=1, source_target_pairs={{0,8},{8,16},{16,24},{24,32},{32,40},{40,48},{48,56},{56,64},{64,7... | collective-permute-start | bytes 393224 | tf_op jit(solution)/shard_map/while/body/eval_jaxpr/ppermute | solution.py:28
  387.6 8.2 %collective-permute-start = (f32[1,1,2048]{2,1,0:T(1,128)S(1)}, f32[1,1,2048]{2,1,0:T(1,128)S(1)}, u32[]{:S(2)}, u32[]{:S(2)}) collective-permute-start(f32[1,1,2048]{2,1,0:T(1,128)S(1)} %get-tuple-element.285), channel_id=1, source_target_pairs={{1,0},{2,1},{3,2},{4,3},{5,4},{6,5},{7,6},{9,8},{10,9},{11,10},{12... | collective-permute-start | bytes 24584 | tf_op jit(solution)/shard_map/while/body/eval_jaxpr/ppermute | solution.py:21
  397.5 8.1 %collective-permute-start.2 = (f32[1,16,2048]{2,1,0:T(8,128)S(1)}, f32[1,16,2048]{2,1,0:T(8,128)S(1)}, u32[]{:S(2)}, u32[]{:S(2)}) collective-permute-start(f32[1,16,2048]{2,1,0:T(8,128)S(1)} %fusion.145), channel_id=1, source_target_pairs={{0,8},{8,16},{16,24},{24,32},{32,40},{40,48},{48,56},{56,64},{64,7... | collective-permute-start | bytes 393224 | tf_op jit(solution)/shard_map/while/body/eval_jaxpr/ppermute | solution.py:28
  405.6 8.2 %collective-permute-start = (f32[1,1,2048]{2,1,0:T(1,128)S(1)}, f32[1,1,2048]{2,1,0:T(1,128)S(1)}, u32[]{:S(2)}, u32[]{:S(2)}) collective-permute-start(f32[1,1,2048]{2,1,0:T(1,128)S(1)} %get-tuple-element.285), channel_id=1, source_target_pairs={{1,0},{2,1},{3,2},{4,3},{5,4},{6,5},{7,6},{9,8},{10,9},{11,10},{12... | collective-permute-start | bytes 24584 | tf_op jit(solution)/shard_map/while/body/eval_jaxpr/ppermute | solution.py:21
  423.7 8.2 %collective-permute-start = (f32[1,1,2048]{2,1,0:T(1,128)S(1)}, f32[1,1,2048]{2,1,0:T(1,128)S(1)}, u32[]{:S(2)}, u32[]{:S(2)}) collective-permute-start(f32[1,1,2048]{2,1,0:T(1,128)S(1)} %get-tuple-element.285), channel_id=1, source_target_pairs={{1,0},{2,1},{3,2},{4,3},{5,4},{6,5},{7,6},{9,8},{10,9},{11,10},{12... | collective-permute-start | bytes 24584 | tf_op jit(solution)/shard_map/while/body/eval_jaxpr/ppermute | solution.py:21
  441.7 8.2 %collective-permute-start = (f32[1,1,2048]{2,1,0:T(1,128)S(1)}, f32[1,1,2048]{2,1,0:T(1,128)S(1)}, u32[]{:S(2)}, u32[]{:S(2)}) collective-permute-start(f32[1,1,2048]{2,1,0:T(1,128)S(1)} %get-tuple-element.285), channel_id=1, source_target_pairs={{1,0},{2,1},{3,2},{4,3},{5,4},{6,5},{7,6},{9,8},{10,9},{11,10},{12... | collective-permute-start | bytes 24584 | tf_op jit(solution)/shard_map/while/body/eval_jaxpr/ppermute | solution.py:21
  459.8 8.2 %collective-permute-start.34 = (f32[1,1,2048]{2,1,0:T(1,128)S(1)}, f32[1,1,2048]{2,1,0:T(1,128)S(1)}, u32[]{:S(2)}, u32[]{:S(2)}) collective-permute-start(f32[1,1,2048]{2,1,0:T(1,128)S(1)} %get-tuple-element.228), channel_id=1, source_target_pairs={{0,1},{1,2},{2,3},{3,4},{4,5},{5,6},{6,7},{8,9},{9,10},{10,11},{11... | collective-permute-start | bytes 24584 | tf_op jit(solution)/shard_map/ppermute | solution.py:18
  (62 other events, 528.8 us)
where the time goes:
time: 499 us; the launch traced here: 496 us
  waiting for transfers between devices  246 us (49%)
  starting transfers between devices  228 us (46%)
  other arithmetic  17.2 us (3%)
    ppermute x23, waiting for transfers between devices, from_behind(): lax.ppermute(array, axis, [(i, (i + by) % peers) for i in range(peers)])  168 us
    ppermute x31, starting transfers between devices, padded_2(): lax.ppermute(lax.slice_in_dim(block, block.shape[dim] - width, None, axis...  147 us
    ppermute x31, starting transfers between devices, padded_2(): lax.ppermute(lax.slice_in_dim(block, 0, width, axis=dim), axis, backward)  78.6 us
    ppermute x31, waiting for transfers between devices, padded_2(): lax.ppermute(lax.slice_in_dim(block, 0, width, axis=dim), axis, backward)  56.7 us
    ppermute x31, waiting for transfers between devices, padded_2(): lax.ppermute(lax.slice_in_dim(block, block.shape[dim] - width, None, axis...  21.3 us
  transfers between devices with their start and end apart: 85, of which 52 were waited for; matrix products, arithmetic and copies ran while one was open for 1% of the time, Pallas kernels for 0%

commit v1 on v0

v1 whole, which is shorter than its diff:
```python
import functools

import jax
import jax.numpy as jnp
from jax import lax
from jax.experimental import pallas as pl
from jax.experimental.pallas import tpu as pltpu
from jax.sharding import PartitionSpec as P

MESH = pl.DeviceIdType.MESH
F32 = jnp.float32
DIFFUSION = 0.03
STEP = 0.02

OWN = 16
BUF = 24
LANES = 128
GROUP = 4
PAIRS = (4, 2, 1)

_names = [
    ("v0", 3), ("dif", 3), ("gro", 3), ("ge0", 3), ("go0", 3),
    ("o1_0", 3), ("o1_1", 3), ("ge1", 3), ("go1", 3), ("go2", 3),
    ("po0", 3), ("po1", 3), ("po2", 3), ("pr0", 3), ("pr1", 3),
    ("ga", 12), ("gb", 12), ("vin", 3), ("vr", 12), ("old", 12),
]
SEM = {}
_at = 0
for _name, _count in _names:
    SEM[_name] = _at
    _at += _count
N_SEM = _at


def kernel(n_t, n_s, cols, ini, src, dif, gro, out, v0, ge0, ge1, ge2, go0, go1, go2, o10, o11, o12,
           po, pr, ee, ne, ob, ps, dd, rr, aa, bb, xa, xb, xv, ga, gb, vin, vo, ap, bp, vr, res,
           ss, rs, ls):
    ge, go, o1 = (ge0, ge1, ge2), (go0, go1, go2), (o10, o11, o12)
    width = cols // GROUP
    wide = width + LANES
    t, s = lax.axis_index("tm"), lax.axis_index("space")
    z, q = t // GROUP, lax.rem(t, GROUP)
    nz = n_t // GROUP
    following = lax.rem(t + 1, n_t)
    has_up, has_down = s > 0, s < n_s - 1
    sent = []

    def when(cond, fn):
        if cond is None:
            fn()
        else:
            pl.when(cond)(fn)

    def both(a, b):
        return b if a is None else (a if b is None else jnp.logical_and(a, b))

    def send(source, target, si, ri, tm, space, cond=None):
        def copy():
            return pltpu.make_async_remote_copy(
                src_ref=source, dst_ref=target, send_sem=ss.at[si], recv_sem=rs.at[ri],
                device_id={"tm": tm, "space": space}, device_id_type=MESH)
        when(cond, lambda: copy().start())
        sent.append((cond, copy))

    def send_edges(source, target, h, si, ri, tm, cond=None):
        send(source(OWN - h, h), target(BUF - h, h), si + 1, ri + 1, tm, s + 1, both(cond, has_down))
        send(source(0, h), target(OWN, h), si + 2, ri + 2, tm, s - 1, both(cond, has_up))

    def arrived(target, ri, cond=None):
        def wait():
            pltpu.make_async_remote_copy(
                src_ref=target, dst_ref=target, send_sem=ss.at[0], recv_sem=rs.at[ri],
                device_id={"tm": following, "space": s}, device_id_type=MESH).wait_recv()
        when(cond, wait)

    def edges_arrived(target, h, ri):
        arrived(target(BUF - h, h), ri + 1, has_up)
        arrived(target(OWN, h), ri + 2, has_down)

    def all_arrived(target, h, ri):
        arrived(target(0, OWN), ri)
        edges_arrived(target, h, ri)

    def rows_of(ref, *lead):
        return lambda r, h: ref.at[(*lead, pl.ds(r, h), slice(None))]

    loads = []

    def load(source, target):
        copy = pltpu.make_async_copy(source, target, ls.at[len(loads)])
        copy.start()
        loads.append(copy)

    for j in range(4):
        load(ini.at[2 * j], v0.at[j, 0:OWN, :])
    load(dif, dd.at[0:OWN, :])
    load(gro, rr.at[0:OWN, :])
    for j in range(4):
        load(src.at[2 * j], ge0.at[j, 0:OWN, :])
        load(src.at[2 * j + 1], go0.at[j, 0:OWN, :])

    def clear():
        for ref in (v0, ge0, ge1, ge2, go0, go1, go2, o10, o11, o12, po, pr, ga, gb, vr):
            for j in range(ref.shape[0]):
                ref[j, OWN:BUF, :] = jnp.zeros((BUF - OWN, ref.shape[2]), F32)
        for ref in (dd, rr, vin):
            ref[OWN:BUF, :] = jnp.zeros((BUF - OWN, ref.shape[1]), F32)

    pl.when(jnp.logical_or(s == 0, s == n_s - 1))(clear)

    barrier = pltpu.get_barrier_semaphore()
    peers = GROUP * 2 * (1 + has_up.astype(jnp.int32) + has_down.astype(jnp.int32)) - 1
    for back in range(2):
        zz = lax.rem(z + nz - back, nz)
        for k in range(GROUP):
            for ds, cond in ((0, None if back else q != k), (1, has_down), (-1, has_up)):
                def greet(zz=zz, k=k, ds=ds):
                    pl.semaphore_signal(barrier, inc=1, device_id={"tm": zz * GROUP + k, "space": s + ds},
                                        device_id_type=MESH)
                when(cond, greet)

    for copy in loads[:6]:
        copy.wait()
    pl.semaphore_wait(barrier, peers)

    def lead(ref, n):
        return lambda r, h: ref.at[0:n, pl.ds(r, h), :]

    def exchange(ref, h, name):
        send_edges(ref, ref, h, SEM[name], SEM[name], t)

    exchange(lead(v0, 4), 1, "v0")
    exchange(rows_of(dd), 4, "dif")
    exchange(rows_of(rr), 4, "gro")
    for copy in loads[6:]:
        copy.wait()
    exchange(lead(ge0, 4), 2, "ge0")
    exchange(lead(go0, 4), 1, "go0")

    lane = lax.broadcasted_iota(jnp.int32, (BUF, LANES), 1)

    def spread(get, c, rows):
        c0 = c * width
        u = get(c0, width)
        west, east = pltpu.roll(u, 1, 1), pltpu.roll(u, width - 1, 1)
        before = pltpu.roll(get(c0 - LANES, LANES), 1, 1) if c > 0 else jnp.zeros((BUF, LANES), F32)
        after = pltpu.roll(get(c0 + width, LANES), LANES - 1, 1) if c < GROUP - 1 else jnp.zeros((BUF, LANES), F32)
        first = jnp.where(lane == 0, before, west[:, :LANES])
        last = jnp.where(lane == LANES - 1, after, east[:, width - LANES:])
        if width > LANES:
            west = jnp.concatenate([first, west[:, LANES:]], axis=1)
            east = jnp.concatenate([east[:, :width - LANES], last], axis=1)
        else:
            west, east = first, last
        north, south = pltpu.roll(u, 1, 0), pltpu.roll(u, BUF - 1, 0)
        u = u[:rows]
        beside = north[:rows] + south[:rows] + west[:rows] + east[:rows]
        n = aa[0:rows, c0:c0 + width] * (beside - 4.0 * u) + bb[0:rows, c0:c0 + width] * u / (1.0 + u * u)
        return n, u

    def cut(c):
        return slice(c * width, (c + 1) * width)

    def field(ref, *lead):
        return lambda c0, w: ref[(*lead, slice(None), slice(c0, c0 + w))]

    def relax(level, j, source, odd_at):
        f = 2.0 ** level
        for c in range(GROUP):
            n, u = spread(source, c, BUF)
            ee[j, :, cut(c)] = u + f * n + ge[level][j, :, cut(c)]
        for c in range(GROUP):
            n, u = spread(field(ee, j), c, BUF)
            ne[j, :, cut(c)] = n
            ob[:, cut(c)] = u + f * n + go[level][j, :, cut(c)]
        for c in range(GROUP):
            n, u = spread(field(ob), c, OWN)
            pair = u + f * n - ee[j, 0:OWN, cut(c)] - 2.0 * f * ne[j, 0:OWN, cut(c)]
            ps[odd_at, :, cut(c)] = pair

    own = slice(0, OWN)

    edges_arrived(rows_of(dd), 4, SEM["dif"])
    edges_arrived(rows_of(rr), 4, SEM["gro"])
    aa[...] = DIFFUSION * dd[...]
    bb[...] = STEP * rr[...]
    edges_arrived(lead(v0, 4), 1, SEM["v0"])

    def first_odd(j):
        for c in range(GROUP):
            n, u = spread(field(v0, j), c, OWN)
            o10[j, own, cut(c)] = u + n + go0[j, own, cut(c)]

    def send_next(source, target, h, name, cond=None):
        send(source(0, OWN), target(0, OWN), SEM[name], SEM[name], following, s)
        send_edges(source, target, h, SEM[name], SEM[name], following)

    first_odd(3)
    send_next(rows_of(o10, 3), rows_of(po, 0), 3, "po0")
    lax.fori_loop(0, 3, lambda j, x: (first_odd(j), x)[1], 0)
    exchange(lead(o10, 3), 3, "o1_0")

    def stage(get, target):
        for k in range(GROUP):
            main = get(k * width, width)
            right = get((k + 1) * width, LANES) if k < GROUP - 1 else jnp.zeros((OWN, LANES), F32)
            left = get(k * width - LANES, LANES) if k > 0 else jnp.zeros((OWN, LANES), F32)
            target[k, :, 0:width] = main
            target[k, :, width:wide] = jnp.where(lane[:OWN] < LANES // 2, right, left)

    def send_group(source, target, h, si, ri, group, itself):
        for k in range(GROUP):
            tm = group * GROUP + k
            me = jnp.logical_and(itself, q == k)

            def keep(k=k):
                pltpu.make_async_copy(source(k)(0, OWN), target(0, OWN), rs.at[ri]).start()
            pl.when(me)(keep)
            send(source(k)(0, OWN), target(0, OWN), si + 3 * k, ri, tm, s, jnp.logical_not(me))
            send_edges(source(k), target, h, si + 3 * k, ri, tm)

    stage(lambda c0, w: ge0[0, own, c0:c0 + w], xa)
    send_group(lambda k: rows_of(xa, k), rows_of(ga, q), 4, SEM["ga"], SEM["ga"] + 3 * q, z, q >= 0)

    edges_arrived(lead(ge0, 4), 2, SEM["ge0"])
    edges_arrived(lead(go0, 4), 1, SEM["go0"])
    edges_arrived(lead(o10, 3), 3, SEM["o1_0"])

    def inner0(j, x):
        relax(0, j + 1, lambda c0, w: o10[j, :, c0:c0 + w], j + 1)
        return x

    lax.fori_loop(0, 3, inner0, 0)
    send_next(rows_of(ps, 3), rows_of(pr, 0), 2, "pr0")
    for c in range(GROUP):
        g = ge0[3, own, cut(c)] + ps[2, :, cut(c)]
        go1[1, own, cut(c)] = g
        o11[1, own, cut(c)] = ee[2, own, cut(c)] + 2.0 * ne[2, own, cut(c)] + g
    send_next(rows_of(o11, 1), rows_of(po, 1), 3, "po1")
    for c in range(GROUP):
        ge1[1, own, cut(c)] = ge0[2, own, cut(c)] + ps[1, :, cut(c)]
    exchange(rows_of(ge1, 1), 2, "ge1")

    all_arrived(rows_of(po, 0), 3, SEM["po0"])
    relax(0, 0, field(po, 0), 0)
    for c in range(GROUP):
        g = ge0[1, own, cut(c)] + ps[0, :, cut(c)]
        go1[0, own, cut(c)] = g
        o11[0, own, cut(c)] = ee[0, own, cut(c)] + 2.0 * ne[0, own, cut(c)] + g
    exchange(rows_of(o11, 0), 3, "o1_1")
    exchange(lead(go1, 2), 1, "go1")

    edges_arrived(rows_of(ge1, 1), 2, SEM["ge1"])
    edges_arrived(rows_of(o11, 0), 3, SEM["o1_1"])
    edges_arrived(lead(go1, 2), 1, SEM["go1"])
    relax(1, 1, field(o11, 0), 5)
    send_next(rows_of(ps, 5), rows_of(pr, 1), 2, "pr1")
    all_arrived(rows_of(pr, 0), 2, SEM["pr0"])
    ge1[0] = ge0[0] + pr[0]
    all_arrived(rows_of(po, 1), 3, SEM["po1"])
    relax(1, 0, field(po, 1), 4)
    for c in range(GROUP):
        g = ge1[1, own, cut(c)] + ps[4, :, cut(c)]
        go2[0, own, cut(c)] = g
        o12[0, own, cut(c)] = ee[0, own, cut(c)] + 4.0 * ne[0, own, cut(c)] + g
    send_next(rows_of(o12, 0), rows_of(po, 2), 3, "po2")
    exchange(rows_of(go2, 0), 2, "go2")

    all_arrived(rows_of(pr, 1), 2, SEM["pr1"])
    ge2[0] = ge1[0] + pr[1]
    edges_arrived(rows_of(go2, 0), 2, SEM["go2"])
    all_arrived(rows_of(po, 2), 3, SEM["po2"])
    relax(2, 0, field(po, 2), 6)

    stage(lambda c0, w: ps[3, :, c0:c0 + w] + ps[5, :, c0:c0 + w] + ps[6, :, c0:c0 + w], xb)
    k_next = lax.rem(following, GROUP)
    z_next = following // GROUP
    send_group(lambda k: rows_of(xb, k), rows_of(gb, k_next), 4, SEM["gb"], SEM["gb"] + 3 * k_next, z_next,
               q < GROUP - 1)

    is_last = t == n_t - 1
    stage(lambda c0, w: ee[0, own, c0:c0 + w], xv)
    for k in range(GROUP):
        tm = lax.rem(following + k, n_t)
        send(xv.at[k], vin.at[0:OWN, :], SEM["old"] + 3 * k, SEM["vin"], tm, s, is_last)
        send_edges(rows_of(xv, k), rows_of(vin), 4, SEM["old"] + 3 * k, SEM["vin"], tm, is_last)

    def own_part(k):
        for whole, part in ((aa, ap), (bb, bp)):
            zero = jnp.zeros((BUF, LANES), F32)
            right = whole[:, (k + 1) * width:(k + 1) * width + LANES] if k < GROUP - 1 else zero
            left = whole[:, k * width - LANES:k * width] if k > 0 else zero
            part[:, 0:width] = whole[:, k * width:(k + 1) * width]
            part[:, width:wide] = jnp.where(lane < LANES // 2, right, left)

    for k in range(GROUP):
        pl.when(q == k)(functools.partial(own_part, k))

    f = 2.0 ** (len(PAIRS))
    all_arrived(rows_of(vin), 4, SEM["vin"])
    for k in range(GROUP):
        all_arrived(rows_of(ga, k), 4, SEM["ga"] + 3 * k)
        all_arrived(rows_of(gb, k), 4, SEM["gb"] + 3 * k)
        u = vin[...] if k == 0 else vo[k - 1]
        beside = pltpu.roll(u, 1, 0) + pltpu.roll(u, BUF - 1, 0) + pltpu.roll(u, 1, 1) + pltpu.roll(u, wide - 1, 1)
        n = ap[...] * (beside - 4.0 * u) + bp[...] * u / (1.0 + u * u)
        vo[k] = u + f * n + (ga[k] + gb[k])
        if k == GROUP - 1:
            ongoing = z < nz - 1
            tm = lax.rem(t + GROUP, n_t)
            send(vo.at[k, 0:OWN, :], vin.at[0:OWN, :], SEM["vin"], SEM["vin"], tm, s, ongoing)
            send_edges(rows_of(vo, k), rows_of(vin), 4, SEM["vin"], SEM["vin"], tm, ongoing)

        def block(r, h, k=k):
            return vo.at[k, pl.ds(r, h), 0:width]

        def place(r, h):
            return vr.at[q, pl.ds(r, h), :]

        tm = z * GROUP + k
        me = q == k

        def keep(k=k):
            pltpu.make_async_copy(block(0, OWN), place(0, OWN), rs.at[SEM["vr"] + 3 * q]).start()
        pl.when(me)(keep)
        send(block(0, OWN), place(0, OWN), SEM["vr"] + 3 * k, SEM["vr"] + 3 * q, tm, s, jnp.logical_not(me))
        send_edges(block, place, 4, SEM["vr"] + 3 * k, SEM["vr"] + 3 * q, tm)

    for k in range(GROUP):
        all_arrived(rows_of(vr, k), 4, SEM["vr"] + 3 * k)
    for c in range(GROUP):
        n, u = spread(lambda c0, w: vr[c0 // width, :, c0 % width:c0 % width + w], c, BUF)
        res[0, :, cut(c)] = u[:OWN]
        res[1, :, cut(c)] = (u + n + go0[0, :, cut(c)])[:OWN]
        ee[1, :, cut(c)] = u + 2.0 * n + go1[0, :, cut(c)]
        ee[2, :, cut(c)] = u + 4.0 * n + go2[0, :, cut(c)]
    stores = []

    def store(j):
        copy = pltpu.make_async_copy(res.at[j], out.at[j], ls.at[j])
        copy.start()
        stores.append(copy)

    store(0)
    store(1)
    for c in range(GROUP):
        n, u = spread(field(ee, 2), c, BUF)
        res[4, :, cut(c)] = u[:OWN]
        res[5, :, cut(c)] = (u + n + go0[2, :, cut(c)])[:OWN]
        ee[3, :, cut(c)] = u + 2.0 * n + go1[1, :, cut(c)]
    store(4)
    store(5)
    for j in (1, 3):
        for c in range(GROUP):
            n, u = spread(field(ee, j), c, OWN)
            res[2 * j, :, cut(c)] = u
            res[2 * j + 1, :, cut(c)] = u + n + go0[j, own, cut(c)]
        store(2 * j)
        store(2 * j + 1)
    for copy in stores:
        copy.wait()
    for cond, copy in sent:
        when(cond, lambda copy=copy: copy().wait_send())


def solution(mesh):
    n_t, n_s = mesh.shape["tm"], mesh.shape["space"]

    def body(initial, source, diffusivity, growth):
        cols = initial.shape[2]
        wide = cols // GROUP + LANES

        def full(*n):
            return pltpu.VMEM((*n, BUF, cols), F32)

        def part(*n):
            return pltpu.VMEM((*n, BUF, wide), F32)

        scratch = [
            full(4), full(4), full(2), full(1), full(4), full(2), full(1), full(4), full(2), full(1),
            full(3), full(2), full(4), full(4), full(), pltpu.VMEM((7, OWN, cols), F32),
            full(), full(), full(), full(),
            pltpu.VMEM((GROUP, OWN, wide), F32), pltpu.VMEM((GROUP, OWN, wide), F32), pltpu.VMEM((GROUP, OWN, wide), F32),
            part(GROUP), part(GROUP), part(), part(GROUP), part(), part(),
            pltpu.VMEM((GROUP, BUF, cols // GROUP), F32),
            pltpu.VMEM(initial.shape, F32),
            pltpu.SemaphoreType.DMA((N_SEM,)), pltpu.SemaphoreType.DMA((N_SEM,)), pltpu.SemaphoreType.DMA((14,)),
        ]
        return pl.pallas_call(
            functools.partial(kernel, n_t, n_s, cols),
            out_shape=jax.ShapeDtypeStruct(initial.shape, F32),
            in_specs=[pl.BlockSpec(memory_space=pl.ANY)] * 4,
            out_specs=pl.BlockSpec(memory_space=pl.ANY),
            scratch_shapes=scratch,
            compiler_params=pltpu.CompilerParams(collective_id=0, has_side_effects=True),
        )(initial, source, diffusivity, growth)

    placed = (P("tm", "space", None), P("tm", "space", None), P("space", None), P("space", None))
    return jax.shard_map(body, mesh=mesh, in_specs=placed, out_specs=P("tm", "space", None), check_vma=False)
```

time: 499 us -> 65.8 us (0.13)
  the two profiles are of different devices: /device:TPU:24 before, /device:TPU:99 now
where the time goes in v1:
time: 65.8 us; the launch traced here: 65.5 us
  Pallas kernels  63.2 us (96%)
  local copies, waits for them, and re-layouts  2.3 us (3%)
    pallas_call x1, Pallas kernels, body(): pl.pallas_call(functools.partial(kernel, n_t, n_s, cols), out_shape=jax.S...  63.2 us
    unnamed x1, local copies, waits for them, and re-layouts  2.3 us

profile of v1, /device:TPU:99, one launch (start us, length us, event | category | flops | bytes accessed | tf_op | source)
XLA Modules:
  0.0 65.5 jit_solution(4402194913550821490)
XLA Ops:
  0.0 63.2 %shard_map.46 = f32[8,16,2048]{2,1,0:T(8,128)} custom-call(f32[8,16,2048]{2,1,0:T(8,128)} %ini.1, f32[8,16,2048]{2,1,0:T(8,128)} %src.1, f32[16,2048]{1,0:T(8,128)} %dif.1, f32[16,2048]{1,0:T(8,128)} %gro.1), custom_call_target="tpu_custom_call" | custom-call | tf_op jit(solution)/shard_map/pallas_call | solution.py:389
  63.2 2.3 %copy.6 = f32[8,16,2048]{2,1,0:T(8,128)} copy(f32[8,16,2048]{2,1,0:T(8,128)} %shard_map.46) | data formatting | bytes 2097152

commit v2 on v1

v2 whole, which is shorter than its diff:
```python
import functools

import jax
import jax.numpy as jnp
from jax import lax
from jax.experimental import pallas as pl
from jax.experimental.pallas import tpu as pltpu
from jax.sharding import PartitionSpec as P

MESH = pl.DeviceIdType.MESH
F32 = jnp.float32
DIFFUSION = 0.03
STEP = 0.02

OWN = 16
BUF = 24
DEEP = 32
LANES = 128
CUTS = 4
GROUP = 8
PAIRS = (4, 2, 1)

_names = [
    ("v0", 3), ("dif", 3), ("gro", 3), ("ge0", 3), ("go0", 3), ("dif2", 3), ("gro2", 3), ("pv", 3), ("pg", 3),
    ("o1_0", 3), ("o1_1", 3), ("ge1", 3), ("go1", 3), ("go2", 3),
    ("po1", 3), ("po2", 3), ("pr0", 3), ("pr1", 3),
    ("ga", 24), ("gb", 24), ("vin", 3), ("vr", 24), ("old", 24),
]
SEM = {}
_at = 0
for _name, _count in _names:
    SEM[_name] = _at
    _at += _count
N_SEM = _at


def kernel(n_t, n_s, cols, ini, src, dif, gro, out, v0, ge0, ge1, ge2, go0, go1, go2, o10, o11, o12,
           po, pr, pv, pg, ee, ne, ob, ps, dd, rr, aa, bb, xa, xb, ga, gb, vin, vo, ap, bp, vr, res,
           ss, rs, ls):
    ge, go, o1 = (ge0, ge1, ge2), (go0, go1, go2), (o10, o11, o12)
    span = cols // CUTS
    width = cols // GROUP
    wide = width + LANES
    t, s = lax.axis_index("tm"), lax.axis_index("space")
    z, q = t // GROUP, lax.rem(t, GROUP)

    def holder(group, block):
        return group * GROUP + lax.rem(block + group * (GROUP // 2), GROUP)

    mine = lax.rem(q + z * (GROUP // 2), GROUP)
    following = lax.rem(t + 1, n_t)
    has_up, has_down = s > 0, s < n_s - 1
    sent = []

    def when(cond, fn):
        if cond is None:
            fn()
        else:
            pl.when(cond)(fn)

    def both(a, b):
        return b if a is None else (a if b is None else jnp.logical_and(a, b))

    def send(source, target, si, ri, tm, space, cond=None):
        def copy():
            return pltpu.make_async_remote_copy(
                src_ref=source, dst_ref=target, send_sem=ss.at[si], recv_sem=rs.at[ri],
                device_id={"tm": tm, "space": space}, device_id_type=MESH)
        when(cond, lambda: copy().start())
        sent.append((cond, copy))

    def send_edges(source, target, h, si, ri, tm, cond=None, total=BUF):
        send(source(OWN - h, h), target(total - h, h), si + 1, ri + 1, tm, s + 1, both(cond, has_down))
        send(source(0, h), target(OWN, h), si + 2, ri + 2, tm, s - 1, both(cond, has_up))

    def arrived(target, ri, cond=None):
        def wait():
            pltpu.make_async_remote_copy(
                src_ref=target, dst_ref=target, send_sem=ss.at[0], recv_sem=rs.at[ri],
                device_id={"tm": following, "space": s}, device_id_type=MESH).wait_recv()
        when(cond, wait)

    def edges_arrived(target, h, ri, total=BUF):
        arrived(target(total - h, h), ri + 1, has_up)
        arrived(target(OWN, h), ri + 2, has_down)

    def all_arrived(target, h, ri, total=BUF):
        arrived(target(0, OWN), ri)
        edges_arrived(target, h, ri, total)

    def rows_of(ref, *lead):
        return lambda r, h: ref.at[(*lead, pl.ds(r, h), slice(None))]

    loads = []

    def load(source, target):
        copy = pltpu.make_async_copy(source, target, ls.at[len(loads)])
        copy.start()
        loads.append(copy)

    for j in range(4):
        load(ini.at[2 * j], v0.at[j, 0:OWN, :])
    load(dif, dd.at[0:OWN, :])
    load(gro, rr.at[0:OWN, :])
    for j in range(4):
        load(src.at[2 * j], ge0.at[j, 0:OWN, :])
        load(src.at[2 * j + 1], go0.at[j, 0:OWN, :])

    def clear():
        for ref in (v0, ge0, ge1, ge2, go0, go1, go2, o10, o11, o12, po, pr, ga, gb, vr):
            for j in range(ref.shape[0]):
                ref[j, OWN:, :] = jnp.zeros((ref.shape[1] - OWN, ref.shape[2]), F32)
        for ref in (dd, rr, pv, pg, vin):
            ref[OWN:, :] = jnp.zeros((ref.shape[0] - OWN, ref.shape[1]), F32)

    pl.when(jnp.logical_or(s == 0, s == n_s - 1))(clear)

    barrier = pltpu.get_barrier_semaphore()
    last = q // (GROUP - 1)
    peers = (GROUP + GROUP * last + (1 - z) * (1 - last)) * (
        1 + has_up.astype(jnp.int32) + has_down.astype(jnp.int32)) - 1

    def greet(tm, cond_here=None, cond=None):
        for ds, there in ((0, cond_here), (1, has_down), (-1, has_up)):
            when(both(cond, there), lambda ds=ds: pl.semaphore_signal(
                barrier, inc=1, device_id={"tm": tm, "space": s + ds}, device_id_type=MESH))

    greet(lax.rem(z * GROUP + n_t - 1, n_t))
    greet(mine, None, jnp.logical_and(z == 1, mine < GROUP - 1))
    for k in range(GROUP):
        greet(z * GROUP + k, q != k)

    for copy in loads[:6]:
        copy.wait()
    pl.semaphore_wait(barrier, peers)

    def lead(ref, n):
        return lambda r, h: ref.at[0:n, pl.ds(r, h), :]

    def exchange(ref, h, name):
        send_edges(ref, ref, h, SEM[name], SEM[name], t)

    def send_next(source, target, h, name):
        send_edges(source, target, h, SEM[name], SEM[name], following)
        send(source(0, OWN), target(0, OWN), SEM[name], SEM[name], following, s)

    exchange(lead(v0, 3), 1, "v0")
    send_next(rows_of(v0, 3), rows_of(pv), 4, "pv")
    for copy in loads[6:]:
        copy.wait()
    send_next(rows_of(go0, 3), rows_of(pg), 3, "pg")
    send_edges(rows_of(dd), rows_of(dd), 4, SEM["dif"], SEM["dif"], t, None, DEEP)
    send_edges(rows_of(rr), rows_of(rr), 4, SEM["gro"], SEM["gro"], t, None, DEEP)

    lane = lax.broadcasted_iota(jnp.int32, (BUF, LANES), 1)

    def spread(get, c, rows):
        c0 = c * span
        u = get(c0, span)
        west, east = pltpu.roll(u, 1, 1), pltpu.roll(u, span - 1, 1)
        before = pltpu.roll(get(c0 - LANES, LANES), 1, 1) if c > 0 else jnp.zeros((BUF, LANES), F32)
        after = pltpu.roll(get(c0 + span, LANES), LANES - 1, 1) if c < CUTS - 1 else jnp.zeros((BUF, LANES), F32)
        first = jnp.where(lane == 0, before, west[:, :LANES])
        last = jnp.where(lane == LANES - 1, after, east[:, span - LANES:])
        if span > LANES:
            west = jnp.concatenate([first, west[:, LANES:]], axis=1)
            east = jnp.concatenate([east[:, :span - LANES], last], axis=1)
        else:
            west, east = first, last
        north, south = pltpu.roll(u, 1, 0), pltpu.roll(u, BUF - 1, 0)
        u = u[:rows]
        beside = north[:rows] + south[:rows] + west[:rows] + east[:rows]
        n = aa[0:rows, c0:c0 + span] * (beside - 4.0 * u) + bb[0:rows, c0:c0 + span] * u / (1.0 + u * u)
        return n, u

    def cut(c):
        return slice(c * span, (c + 1) * span)

    def field(ref, *lead):
        return lambda c0, w: ref[(*lead, slice(None), slice(c0, c0 + w))]

    def relax(level, j, source, odd_at):
        f = 2.0 ** level
        for c in range(CUTS):
            n, u = spread(source, c, BUF)
            ee[j, :, cut(c)] = u + f * n + ge[level][j, :, cut(c)]
        for c in range(CUTS):
            n, u = spread(field(ee, j), c, BUF)
            ne[j, :, cut(c)] = n
            ob[:, cut(c)] = u + f * n + go[level][j, :, cut(c)]
        for c in range(CUTS):
            n, u = spread(field(ob), c, OWN)
            pair = u + f * n - ee[j, 0:OWN, cut(c)] - 2.0 * f * ne[j, 0:OWN, cut(c)]
            ps[odd_at, :, cut(c)] = pair

    own = slice(0, OWN)

    edges_arrived(lead(v0, 3), 1, SEM["v0"])
    aa[own] = DIFFUSION * dd[own]
    bb[own] = STEP * rr[own]

    def first_odd(j):
        for c in range(CUTS):
            n, u = spread(field(v0, j), c, OWN)
            o10[j, own, cut(c)] = u + n + go0[j, own, cut(c)]

    lax.fori_loop(0, 3, lambda j, x: (first_odd(j), x)[1], 0)
    exchange(lead(o10, 3), 3, "o1_0")
    exchange(lead(ge0, 4), 2, "ge0")
    exchange(lead(go0, 4), 1, "go0")
    for ref, name in ((dd, "dif2"), (rr, "gro2")):
        send(ref.at[8:12, :], ref.at[24:28, :], SEM[name] + 1, SEM[name] + 1, t, s + 1, has_down)
        send(ref.at[4:8, :], ref.at[20:24, :], SEM[name] + 2, SEM[name] + 2, t, s - 1, has_up)

    def stage(get, target):
        for k in range(GROUP):
            main = get(k * width, width)
            right = get((k + 1) * width, LANES) if k < GROUP - 1 else jnp.zeros((OWN, LANES), F32)
            left = get(k * width - LANES, LANES) if k > 0 else jnp.zeros((OWN, LANES), F32)
            target[k, :, 0:width] = main
            target[k, :, width:wide] = jnp.where(lane[:OWN] < LANES // 2, right, left)

    def send_group(source, target, si, ri, group, itself, cond=None):
        for k in range(GROUP):
            tm = holder(group, k)
            me = jnp.logical_and(itself, mine == k)

            def keep(k=k):
                pltpu.make_async_copy(source(k)(0, OWN), target(0, OWN), rs.at[ri]).start()
            pl.when(me)(keep)
            send_edges(source(k), target, 8, si + 3 * k, ri, tm, cond, DEEP)
            send(source(k)(0, OWN), target(0, OWN), si + 3 * k, ri, tm, s, both(cond, jnp.logical_not(me)))

    edges_arrived(rows_of(dd), 4, SEM["dif"], DEEP)
    edges_arrived(rows_of(rr), 4, SEM["gro"], DEEP)
    for r, at in ((OWN, OWN), (BUF - 4, DEEP - 4)):
        aa[r:r + 4] = DIFFUSION * dd[at:at + 4]
        bb[r:r + 4] = STEP * rr[at:at + 4]
    edges_arrived(lead(o10, 3), 3, SEM["o1_0"])
    edges_arrived(lead(ge0, 4), 2, SEM["ge0"])
    edges_arrived(lead(go0, 4), 1, SEM["go0"])

    relax(0, 2, field(o10, 1), 2)
    for c in range(CUTS):
        g = ge0[3, own, cut(c)] + ps[2, :, cut(c)]
        go1[1, own, cut(c)] = g
        o11[1, own, cut(c)] = ee[2, own, cut(c)] + 2.0 * ne[2, own, cut(c)] + g
    send_next(rows_of(o11, 1), rows_of(po, 1), 3, "po1")
    relax(0, 3, field(o10, 2), 3)
    send_next(rows_of(ps, 3), rows_of(pr, 0), 2, "pr0")
    relax(0, 1, field(o10, 0), 1)
    for c in range(CUTS):
        ge1[1, own, cut(c)] = ge0[2, own, cut(c)] + ps[1, :, cut(c)]
    exchange(rows_of(ge1, 1), 2, "ge1")

    all_arrived(rows_of(pv), 4, SEM["pv"])
    all_arrived(rows_of(pg), 3, SEM["pg"])
    for c in range(CUTS):
        n, u = spread(field(pv), c, BUF)
        po[0, :, cut(c)] = u + n + pg[:, cut(c)]
    relax(0, 0, field(po, 0), 0)
    for c in range(CUTS):
        g = ge0[1, own, cut(c)] + ps[0, :, cut(c)]
        go1[0, own, cut(c)] = g
        o11[0, own, cut(c)] = ee[0, own, cut(c)] + 2.0 * ne[0, own, cut(c)] + g
    exchange(rows_of(o11, 0), 3, "o1_1")
    exchange(lead(go1, 2), 1, "go1")
    stage(lambda c0, w: ge0[0, own, c0:c0 + w], xa)
    send_group(lambda k: rows_of(xa, k), rows_of(ga, q), SEM["ga"], SEM["ga"] + 3 * q, z, q >= 0)

    edges_arrived(rows_of(ge1, 1), 2, SEM["ge1"])
    edges_arrived(rows_of(o11, 0), 3, SEM["o1_1"])
    edges_arrived(lead(go1, 2), 1, SEM["go1"])
    relax(1, 1, field(o11, 0), 5)
    send_next(rows_of(ps, 5), rows_of(pr, 1), 2, "pr1")
    all_arrived(rows_of(pr, 0), 2, SEM["pr0"])
    ge1[0] = ge0[0] + pr[0]
    all_arrived(rows_of(po, 1), 3, SEM["po1"])
    relax(1, 0, field(po, 1), 4)
    for c in range(CUTS):
        g = ge1[1, own, cut(c)] + ps[4, :, cut(c)]
        go2[0, own, cut(c)] = g
        o12[0, own, cut(c)] = ee[0, own, cut(c)] + 4.0 * ne[0, own, cut(c)] + g
    send_next(rows_of(o12, 0), rows_of(po, 2), 3, "po2")
    exchange(rows_of(go2, 0), 2, "go2")

    all_arrived(rows_of(pr, 1), 2, SEM["pr1"])
    ge2[0] = ge1[0] + pr[1]
    edges_arrived(rows_of(go2, 0), 2, SEM["go2"])
    all_arrived(rows_of(po, 2), 3, SEM["po2"])
    relax(2, 0, field(po, 2), 6)

    is_last = t == n_t - 1

    def onward(c0, w):
        at = slice(c0, c0 + w)
        pairs = ps[3, :, at] + ps[5, :, at] + ps[6, :, at]
        return pairs + jnp.where(is_last, ee[0, own, at] + 8.0 * ne[0, own, at], 0.0)

    stage(onward, xb)
    for k in range(GROUP):
        tm = lax.rem(following + k, n_t)
        send_edges(rows_of(xb, k), rows_of(vin), 8, SEM["old"] + 3 * k, SEM["vin"], tm, is_last, DEEP)
        send(xb.at[k], vin.at[0:OWN, :], SEM["old"] + 3 * k, SEM["vin"], tm, s, is_last)
    k_next = lax.rem(following, GROUP)
    z_next = following // GROUP
    send_group(lambda k: rows_of(xb, k), rows_of(gb, k_next), SEM["gb"], SEM["gb"] + 3 * k_next, z_next,
               q < GROUP - 1, jnp.logical_not(is_last))

    for ref, name in ((dd, "dif2"), (rr, "gro2")):
        arrived(ref.at[24:28, :], SEM[name] + 1, has_up)
        arrived(ref.at[20:24, :], SEM[name] + 2, has_down)
    lane_deep = lax.broadcasted_iota(jnp.int32, (DEEP, LANES), 1)

    def own_part(k):
        for whole, part, scale in ((dd, ap, DIFFUSION), (rr, bp, STEP)):
            zero = jnp.zeros((DEEP, LANES), F32)
            right = whole[:, (k + 1) * width:(k + 1) * width + LANES] if k < GROUP - 1 else zero
            left = whole[:, k * width - LANES:k * width] if k > 0 else zero
            part[:, 0:width] = scale * whole[:, k * width:(k + 1) * width]
            part[:, width:wide] = scale * jnp.where(lane_deep < LANES // 2, right, left)

    for k in range(GROUP):
        pl.when(mine == k)(functools.partial(own_part, k))

    f = 2.0 ** (len(PAIRS))
    all_arrived(rows_of(vin), 8, SEM["vin"], DEEP)
    for k in range(GROUP):
        all_arrived(rows_of(ga, k), 8, SEM["ga"] + 3 * k, DEEP)
        if k == 0:
            arrived(gb.at[0, 0:OWN, :], SEM["gb"], z == 1)
            arrived(gb.at[0, DEEP - 8:DEEP, :], SEM["gb"] + 1, jnp.logical_and(z == 1, has_up))
            arrived(gb.at[0, OWN:OWN + 8, :], SEM["gb"] + 2, jnp.logical_and(z == 1, has_down))
        else:
            all_arrived(rows_of(gb, k), 8, SEM["gb"] + 3 * k, DEEP)
        u = vin[...] if k == 0 else vo[k - 1]
        beside = pltpu.roll(u, 1, 0) + pltpu.roll(u, DEEP - 1, 0) + pltpu.roll(u, 1, 1) + pltpu.roll(u, wide - 1, 1)
        n = ap[...] * (beside - 4.0 * u) + bp[...] * u / (1.0 + u * u)
        u = u + f * n + gb[k]
        if k == 0:
            u = jnp.where(z == 0, vin[...], u)
        vo[k] = u + ga[k]
        if k == GROUP - 1:
            tm = holder(1, mine)
            send_edges(rows_of(vo, k), rows_of(vin), 8, SEM["vin"], SEM["vin"], tm, z == 0, DEEP)
            send(vo.at[k, 0:OWN, :], vin.at[0:OWN, :], SEM["vin"], SEM["vin"], tm, s, z == 0)

        def block(r, h, k=k):
            return vo.at[k, pl.ds(r, h), 0:width]

        place = rows_of(vr, mine)
        tm = z * GROUP + k
        me = q == k

        def keep():
            pltpu.make_async_copy(block(0, OWN), place(0, OWN), rs.at[SEM["vr"] + 3 * mine]).start()
        pl.when(me)(keep)
        send_edges(block, place, 4, SEM["vr"] + 3 * k, SEM["vr"] + 3 * mine, tm)
        send(block(0, OWN), place(0, OWN), SEM["vr"] + 3 * k, SEM["vr"] + 3 * mine, tm, s, jnp.logical_not(me))

    for k in range(GROUP):
        all_arrived(rows_of(vr, k), 4, SEM["vr"] + 3 * k)

    def returned(c0, w):
        if w <= width:
            return vr[c0 // width, :, c0 % width:c0 % width + w]
        return jnp.concatenate([vr[c0 // width + i] for i in range(w // width)], axis=1)

    for c in range(CUTS):
        n, u = spread(returned, c, BUF)
        res[0, :, cut(c)] = u[:OWN]
        res[1, :, cut(c)] = (u + n + go0[0, :, cut(c)])[:OWN]
        ee[1, :, cut(c)] = u + 2.0 * n + go1[0, :, cut(c)]
        ee[2, :, cut(c)] = u + 4.0 * n + go2[0, :, cut(c)]
    stores = []

    def store(j):
        copy = pltpu.make_async_copy(res.at[j], out.at[j], ls.at[j])
        copy.start()
        stores.append(copy)

    store(0)
    store(1)
    for c in range(CUTS):
        n, u = spread(field(ee, 2), c, BUF)
        res[4, :, cut(c)] = u[:OWN]
        res[5, :, cut(c)] = (u + n + go0[2, :, cut(c)])[:OWN]
        ee[3, :, cut(c)] = u + 2.0 * n + go1[1, :, cut(c)]
    store(4)
    store(5)
    for j in (1, 3):
        for c in range(CUTS):
            n, u = spread(field(ee, j), c, OWN)
            res[2 * j, :, cut(c)] = u
            res[2 * j + 1, :, cut(c)] = u + n + go0[j, own, cut(c)]
        store(2 * j)
        store(2 * j + 1)
    for copy in stores:
        copy.wait()
    for cond, copy in sent:
        when(cond, lambda copy=copy: copy().wait_send())


def solution(mesh):
    n_t, n_s = mesh.shape["tm"], mesh.shape["space"]

    def body(initial, source, diffusivity, growth):
        cols = initial.shape[2]
        wide = cols // GROUP + LANES

        def full(*n):
            return pltpu.VMEM((*n, BUF, cols), F32)

        def part(*n):
            return pltpu.VMEM((*n, DEEP, wide), F32)

        scratch = [
            full(4), full(4), full(2), full(1), full(4), full(2), full(1), full(4), full(2), full(1),
            full(3), full(2), full(), full(), full(4), full(4), full(), pltpu.VMEM((7, OWN, cols), F32),
            pltpu.VMEM((DEEP, cols), F32), pltpu.VMEM((DEEP, cols), F32), full(), full(),
            pltpu.VMEM((GROUP, OWN, wide), F32), pltpu.VMEM((GROUP, OWN, wide), F32),
            part(GROUP), part(GROUP), part(), part(GROUP), part(), part(),
            pltpu.VMEM((GROUP, BUF, cols // GROUP), F32),
            pltpu.VMEM(initial.shape, F32),
            pltpu.SemaphoreType.DMA((N_SEM,)), pltpu.SemaphoreType.DMA((N_SEM,)), pltpu.SemaphoreType.DMA((14,)),
        ]
        return pl.pallas_call(
            functools.partial(kernel, n_t, n_s, cols),
            out_shape=jax.ShapeDtypeStruct(initial.shape, F32),
            in_specs=[pl.BlockSpec(memory_space=pl.ANY)] * 4,
            out_specs=pl.BlockSpec(memory_space=pl.ANY),
            scratch_shapes=scratch,
            compiler_params=pltpu.CompilerParams(collective_id=0, has_side_effects=True),
        )(initial, source, diffusivity, growth)

    placed = (P("tm", "space", None), P("tm", "space", None), P("space", None), P("space", None))
    return jax.shard_map(body, mesh=mesh, in_specs=placed, out_specs=P("tm", "space", None), check_vma=False)
```

time: 65.8 us -> 59.8 us (0.909)
  Pallas kernels: 63.2 us -> 57.4 us
    pallas_call x1, Pallas kernels: 63.2 us -> 57.4 us  [body(): pl.pallas_call(functools.partial(kernel, n_t, n_s, cols), out_shape=jax.S...]
where the time goes in v2:
time: 59.8 us; the launch traced here: 59.7 us
  Pallas kernels  57.4 us (96%)
  local copies, waits for them, and re-layouts  2.3 us (4%)
    pallas_call x1, Pallas kernels, body(): pl.pallas_call(functools.partial(kernel, n_t, n_s, cols), out_shape=jax.S...  57.4 us
    unnamed x1, local copies, waits for them, and re-layouts  2.3 us

profile of v2, /device:TPU:99, one launch (start us, length us, event | category | flops | bytes accessed | tf_op | source)
XLA Modules:
  0.0 59.7 jit_solution(10581789049938498401)
XLA Ops:
  0.0 57.4 %shard_map.46 = f32[8,16,2048]{2,1,0:T(8,128)} custom-call(f32[8,16,2048]{2,1,0:T(8,128)} %ini.1, f32[8,16,2048]{2,1,0:T(8,128)} %src.1, f32[16,2048]{1,0:T(8,128)} %dif.1, f32[16,2048]{1,0:T(8,128)} %gro.1), custom_call_target="tpu_custom_call" | custom-call | tf_op jit(solution)/shard_map/pallas_call | solution.py:427
  57.4 2.3 %copy.6 = f32[8,16,2048]{2,1,0:T(8,128)} copy(f32[8,16,2048]{2,1,0:T(8,128)} %shard_map.46) | data formatting | bytes 2097152

commit v3 on v2

--- a/solution.py
+++ b/solution.py
@@ -24,7 +24,7 @@
     ("v0", 3), ("dif", 3), ("gro", 3), ("ge0", 3), ("go0", 3), ("dif2", 3), ("gro2", 3), ("pv", 3), ("pg", 3),
     ("o1_0", 3), ("o1_1", 3), ("ge1", 3), ("go1", 3), ("go2", 3),
     ("po1", 3), ("po2", 3), ("pr0", 3), ("pr1", 3),
-    ("ga", 24), ("gb", 24), ("vin", 3), ("vr", 24), ("old", 24),
+    ("ga", 24), ("gae", 3), ("gb", 24), ("vin", 3), ("vr", 24), ("old", 24),
 ]
 SEM = {}
 _at = 0
@@ -68,6 +68,11 @@
                 device_id={"tm": tm, "space": space}, device_id_type=MESH)
         when(cond, lambda: copy().start())
         sent.append((cond, copy))
+
+    def settle():
+        for cond, copy in sent:
+            when(cond, lambda copy=copy: copy().wait_send())
+        sent.clear()
 
     def send_edges(source, target, h, si, ri, tm, cond=None, total=BUF):
         send(source(OWN - h, h), target(total - h, h), si + 1, ri + 1, tm, s + 1, both(cond, has_down))
@@ -208,9 +213,6 @@
     exchange(lead(o10, 3), 3, "o1_0")
     exchange(lead(ge0, 4), 2, "ge0")
     exchange(lead(go0, 4), 1, "go0")
-    for ref, name in ((dd, "dif2"), (rr, "gro2")):
-        send(ref.at[8:12, :], ref.at[24:28, :], SEM[name] + 1, SEM[name] + 1, t, s + 1, has_down)
-        send(ref.at[4:8, :], ref.at[20:24, :], SEM[name] + 2, SEM[name] + 2, t, s - 1, has_up)
 
     def stage(get, target):
         for k in range(GROUP):
@@ -220,7 +222,7 @@
             target[k, :, 0:width] = main
             target[k, :, width:wide] = jnp.where(lane[:OWN] < LANES // 2, right, left)
 
-    def send_group(source, target, si, ri, group, itself, cond=None):
+    def send_group(source, target, si, ri, group, itself, cond=None, edges=True):
         for k in range(GROUP):
             tm = holder(group, k)
             me = jnp.logical_and(itself, mine == k)
@@ -228,9 +230,12 @@
             def keep(k=k):
                 pltpu.make_async_copy(source(k)(0, OWN), target(0, OWN), rs.at[ri]).start()
             pl.when(me)(keep)
-            send_edges(source(k), target, 8, si + 3 * k, ri, tm, cond, DEEP)
+            if edges:
+                send_edges(source(k), target, 8, si + 3 * k, ri, tm, cond, DEEP)
             send(source(k)(0, OWN), target(0, OWN), si + 3 * k, ri, tm, s, both(cond, jnp.logical_not(me)))
 
+    stage(lambda c0, w: ge0[0, own, c0:c0 + w], xa)
+    send_group(lambda k: rows_of(xa, k), rows_of(ga, q), SEM["ga"], SEM["ga"] + 3 * q, z, q >= 0, None, False)
     edges_arrived(rows_of(dd), 4, SEM["dif"], DEEP)
     edges_arrived(rows_of(rr), 4, SEM["gro"], DEEP)
     for r, at in ((OWN, OWN), (BUF - 4, DEEP - 4)):
@@ -265,9 +270,11 @@
         o11[0, own, cut(c)] = ee[0, own, cut(c)] + 2.0 * ne[0, own, cut(c)] + g
     exchange(rows_of(o11, 0), 3, "o1_1")
     exchange(lead(go1, 2), 1, "go1")
-    stage(lambda c0, w: ge0[0, own, c0:c0 + w], xa)
-    send_group(lambda k: rows_of(xa, k), rows_of(ga, q), SEM["ga"], SEM["ga"] + 3 * q, z, q >= 0)
-
+
+    for k in range(GROUP):
+        arrived(ga.at[k, 0:OWN, :], SEM["ga"] + 3 * k)
+    slots = lambda r, h: ga.at[:, pl.ds(r, h), :]
+    send_edges(slots, slots, 8, SEM["gae"], SEM["gae"], t, None, DEEP)
     edges_arrived(rows_of(ge1, 1), 2, SEM["ge1"])
     edges_arrived(rows_of(o11, 0), 3, SEM["o1_1"])
     edges_arrived(lead(go1, 2), 1, SEM["go1"])
@@ -284,6 +291,9 @@
     send_next(rows_of(o12, 0), rows_of(po, 2), 3, "po2")
     exchange(rows_of(go2, 0), 2, "go2")
 
+    for ref, name in ((dd, "dif2"), (rr, "gro2")):
+        send(ref.at[8:12, :], ref.at[24:28, :], SEM[name] + 1, SEM[name] + 1, t, s + 1, has_down)
+        send(ref.at[4:8, :], ref.at[20:24, :], SEM[name] + 2, SEM[name] + 2, t, s - 1, has_up)
     all_arrived(rows_of(pr, 1), 2, SEM["pr1"])
     ge2[0] = ge1[0] + pr[1]
     edges_arrived(rows_of(go2, 0), 2, SEM["go2"])
@@ -297,6 +307,8 @@
         pairs = ps[3, :, at] + ps[5, :, at] + ps[6, :, at]
         return pairs + jnp.where(is_last, ee[0, own, at] + 8.0 * ne[0, own, at], 0.0)
 
+    earlier = list(sent)
+    sent.clear()
     stage(onward, xb)
     for k in range(GROUP):
         tm = lax.rem(following + k, n_t)
@@ -307,6 +319,11 @@
     send_group(lambda k: rows_of(xb, k), rows_of(gb, k_next), SEM["gb"], SEM["gb"] + 3 * k_next, z_next,
                q < GROUP - 1, jnp.logical_not(is_last))
 
+    later = list(sent)
+    sent[:] = earlier
+    settle()
+    sent[:] = later
+
     for ref, name in ((dd, "dif2"), (rr, "gro2")):
         arrived(ref.at[24:28, :], SEM[name] + 1, has_up)
         arrived(ref.at[20:24, :], SEM[name] + 2, has_down)
@@ -324,9 +341,9 @@
         pl.when(mine == k)(functools.partial(own_part, k))
 
     f = 2.0 ** (len(PAIRS))
+    edges_arrived(slots, 8, SEM["gae"], DEEP)
     all_arrived(rows_of(vin), 8, SEM["vin"], DEEP)
     for k in range(GROUP):
-        all_arrived(rows_of(ga, k), 8, SEM["ga"] + 3 * k, DEEP)
         if k == 0:
             arrived(gb.at[0, 0:OWN, :], SEM["gb"], z == 1)
             arrived(gb.at[0, DEEP - 8:DEEP, :], SEM["gb"] + 1, jnp.logical_and(z == 1, has_up))
@@ -358,6 +375,8 @@
         send_edges(block, place, 4, SEM["vr"] + 3 * k, SEM["vr"] + 3 * mine, tm)
         send(block(0, OWN), place(0, OWN), SEM["vr"] + 3 * k, SEM["vr"] + 3 * mine, tm, s, jnp.logical_not(me))
 
+    settle()
+
     for k in range(GROUP):
         all_arrived(rows_of(vr, k), 4, SEM["vr"] + 3 * k)
 
@@ -397,8 +416,6 @@
         store(2 * j + 1)
     for copy in stores:
         copy.wait()
-    for cond, copy in sent:
-        when(cond, lambda copy=copy: copy().wait_send())
 
 
 def solution(mesh):

time: 59.8 us -> 59.1 us (0.988)
  Pallas kernels: 57.4 us -> 56.7 us
    pallas_call x1, Pallas kernels: 57.4 us -> 56.7 us  [body(): pl.pallas_call(functools.partial(kernel, n_t, n_s, cols), out_shape=jax.S...]
where the time goes in v3:
time: 59.1 us; the launch traced here: 59 us
  Pallas kernels  56.7 us (96%)
  local copies, waits for them, and re-layouts  2.3 us (4%)
    pallas_call x1, Pallas kernels, body(): pl.pallas_call(functools.partial(kernel, n_t, n_s, cols), out_shape=jax.S...  56.7 us
    unnamed x1, local copies, waits for them, and re-layouts  2.3 us

profile of v3, /device:TPU:99, one launch (start us, length us, event | category | flops | bytes accessed | tf_op | source)
XLA Modules:
  0.0 59.0 jit_solution(14210965114395044823)
XLA Ops:
  0.0 56.7 %shard_map.46 = f32[8,16,2048]{2,1,0:T(8,128)} custom-call(f32[8,16,2048]{2,1,0:T(8,128)} %ini.1, f32[8,16,2048]{2,1,0:T(8,128)} %src.1, f32[16,2048]{1,0:T(8,128)} %dif.1, f32[16,2048]{1,0:T(8,128)} %gro.1), custom_call_target="tpu_custom_call" | custom-call | tf_op jit(solution)/shard_map/pallas_call | solution.py:444
  56.7 2.3 %copy.6 = f32[8,16,2048]{2,1,0:T(8,128)} copy(f32[8,16,2048]{2,1,0:T(8,128)} %shard_map.46) | data formatting | bytes 2097152

commit v4 on v3

--- a/solution.py
+++ b/solution.py
@@ -103,6 +103,30 @@
         copy.start()
         loads.append(copy)
 
+    def clear():
+        for ref in (v0, ge0, ge1, ge2, go0, go1, go2, o10, o11, o12, po, pr, ga, gb, vr):
+            for j in range(ref.shape[0]):
+                ref[j, OWN:, :] = jnp.zeros((ref.shape[1] - OWN, ref.shape[2]), F32)
+        for ref in (dd, rr, pv, pg, vin):
+            ref[OWN:, :] = jnp.zeros((ref.shape[0] - OWN, ref.shape[1]), F32)
+
+    pl.when(jnp.logical_or(s == 0, s == n_s - 1))(clear)
+
+    barrier = pltpu.get_barrier_semaphore()
+    last = q // (GROUP - 1)
+    peers = (GROUP + GROUP * last + (1 - z) * (1 - last)) * (
+        1 + has_up.astype(jnp.int32) + has_down.astype(jnp.int32)) - 1
+
+    def greet(tm, cond_here=None, cond=None):
+        for ds, there in ((0, cond_here), (1, has_down), (-1, has_up)):
+            when(both(cond, there), lambda ds=ds: pl.semaphore_signal(
+                barrier, inc=1, device_id={"tm": tm, "space": s + ds}, device_id_type=MESH))
+
+    greet(lax.rem(z * GROUP + n_t - 1, n_t))
+    greet(mine, None, jnp.logical_and(z == 1, mine < GROUP - 1))
+    for k in range(GROUP):
+        greet(z * GROUP + k, q != k)
+
     for j in range(4):
         load(ini.at[2 * j], v0.at[j, 0:OWN, :])
     load(dif, dd.at[0:OWN, :])
@@ -110,30 +134,6 @@
     for j in range(4):
         load(src.at[2 * j], ge0.at[j, 0:OWN, :])
         load(src.at[2 * j + 1], go0.at[j, 0:OWN, :])
-
-    def clear():
-        for ref in (v0, ge0, ge1, ge2, go0, go1, go2, o10, o11, o12, po, pr, ga, gb, vr):
-            for j in range(ref.shape[0]):
-                ref[j, OWN:, :] = jnp.zeros((ref.shape[1] - OWN, ref.shape[2]), F32)
-        for ref in (dd, rr, pv, pg, vin):
-            ref[OWN:, :] = jnp.zeros((ref.shape[0] - OWN, ref.shape[1]), F32)
-
-    pl.when(jnp.logical_or(s == 0, s == n_s - 1))(clear)
-
-    barrier = pltpu.get_barrier_semaphore()
-    last = q // (GROUP - 1)
-    peers = (GROUP + GROUP * last + (1 - z) * (1 - last)) * (
-        1 + has_up.astype(jnp.int32) + has_down.astype(jnp.int32)) - 1
-
-    def greet(tm, cond_here=None, cond=None):
-        for ds, there in ((0, cond_here), (1, has_down), (-1, has_up)):
-            when(both(cond, there), lambda ds=ds: pl.semaphore_signal(
-                barrier, inc=1, device_id={"tm": tm, "space": s + ds}, device_id_type=MESH))
-
-    greet(lax.rem(z * GROUP + n_t - 1, n_t))
-    greet(mine, None, jnp.logical_and(z == 1, mine < GROUP - 1))
-    for k in range(GROUP):
-        greet(z * GROUP + k, q != k)
 
     for copy in loads[:6]:
         copy.wait()
@@ -222,7 +222,7 @@
             target[k, :, 0:width] = main
             target[k, :, width:wide] = jnp.where(lane[:OWN] < LANES // 2, right, left)
 
-    def send_group(source, target, si, ri, group, itself, cond=None, edges=True):
+    def send_group(source, target, si, ri, group, itself, cond=None, edges=None):
         for k in range(GROUP):
             tm = holder(group, k)
             me = jnp.logical_and(itself, mine == k)
@@ -230,12 +230,13 @@
             def keep(k=k):
                 pltpu.make_async_copy(source(k)(0, OWN), target(0, OWN), rs.at[ri]).start()
             pl.when(me)(keep)
-            if edges:
-                send_edges(source(k), target, 8, si + 3 * k, ri, tm, cond, DEEP)
+            if edges is not None:
+                for h, chosen in edges:
+                    send_edges(source(k), target, h, si + 3 * k, ri, tm, both(cond, chosen), DEEP)
             send(source(k)(0, OWN), target(0, OWN), si + 3 * k, ri, tm, s, both(cond, jnp.logical_not(me)))
 
     stage(lambda c0, w: ge0[0, own, c0:c0 + w], xa)
-    send_group(lambda k: rows_of(xa, k), rows_of(ga, q), SEM["ga"], SEM["ga"] + 3 * q, z, q >= 0, None, False)
+    send_group(lambda k: rows_of(xa, k), rows_of(ga, q), SEM["ga"], SEM["ga"] + 3 * q, z, q >= 0)
     edges_arrived(rows_of(dd), 4, SEM["dif"], DEEP)
     edges_arrived(rows_of(rr), 4, SEM["gro"], DEEP)
     for r, at in ((OWN, OWN), (BUF - 4, DEEP - 4)):
@@ -317,7 +318,7 @@
     k_next = lax.rem(following, GROUP)
     z_next = following // GROUP
     send_group(lambda k: rows_of(xb, k), rows_of(gb, k_next), SEM["gb"], SEM["gb"] + 3 * k_next, z_next,
-               q < GROUP - 1, jnp.logical_not(is_last))
+               q < GROUP - 1, jnp.logical_not(is_last), ((7, k_next < 4), (3, k_next >= 4)))
 
     later = list(sent)
     sent[:] = earlier
@@ -346,10 +347,10 @@
     for k in range(GROUP):
         if k == 0:
             arrived(gb.at[0, 0:OWN, :], SEM["gb"], z == 1)
-            arrived(gb.at[0, DEEP - 8:DEEP, :], SEM["gb"] + 1, jnp.logical_and(z == 1, has_up))
-            arrived(gb.at[0, OWN:OWN + 8, :], SEM["gb"] + 2, jnp.logical_and(z == 1, has_down))
+            arrived(gb.at[0, DEEP - 7:DEEP, :], SEM["gb"] + 1, jnp.logical_and(z == 1, has_up))
+            arrived(gb.at[0, OWN:OWN + 7, :], SEM["gb"] + 2, jnp.logical_and(z == 1, has_down))
         else:
-            all_arrived(rows_of(gb, k), 8, SEM["gb"] + 3 * k, DEEP)
+            all_arrived(rows_of(gb, k), 7 if k < 4 else 3, SEM["gb"] + 3 * k, DEEP)
         u = vin[...] if k == 0 else vo[k - 1]
         beside = pltpu.roll(u, 1, 0) + pltpu.roll(u, DEEP - 1, 0) + pltpu.roll(u, 1, 1) + pltpu.roll(u, wide - 1, 1)
         n = ap[...] * (beside - 4.0 * u) + bp[...] * u / (1.0 + u * u)

time: 59.1 us -> 58.8 us (level)
  no operation moved by 1% of the time
where the time goes in v4:
time: 58.8 us; the launch traced here: 58.7 us
  Pallas kernels  56.4 us (96%)
  local copies, waits for them, and re-layouts  2.3 us (4%)
    pallas_call x1, Pallas kernels, body(): pl.pallas_call(functools.partial(kernel, n_t, n_s, cols), out_shape=jax.S...  56.4 us
    unnamed x1, local copies, waits for them, and re-layouts  2.3 us

profile of v4, /device:TPU:99, one launch (start us, length us, event | category | flops | bytes accessed | tf_op | source)
XLA Modules:
  0.0 58.7 jit_solution(14139853502441125059)
XLA Ops:
  0.0 56.4 %shard_map.46 = f32[8,16,2048]{2,1,0:T(8,128)} custom-call(f32[8,16,2048]{2,1,0:T(8,128)} %ini.1, f32[8,16,2048]{2,1,0:T(8,128)} %src.1, f32[16,2048]{1,0:T(8,128)} %dif.1, f32[16,2048]{1,0:T(8,128)} %gro.1), custom_call_target="tpu_custom_call" | custom-call | tf_op jit(solution)/shard_map/pallas_call | solution.py:445
  56.4 2.3 %copy.6 = f32[8,16,2048]{2,1,0:T(8,128)} copy(f32[8,16,2048]{2,1,0:T(8,128)} %shard_map.46) | data formatting | bytes 2097152
